TPU v7x, 256 devices: a whole 4x4x8 slice. The times are simulated.
256 devices in a mesh: tm: 16 (over y, x), sx: 2 (over core), sy: 8 (over z).
Axes of the slice: x: 4, y: 4, z: 8, core: 2. Of those that a mesh axis runs over, the one named last changes fastest.
Arguments:
- frames: bfloat16 [32, 64, 128, 512], P('tm', 'sx', 'sy'), may hold values from -6 to 6
- input_weight: bfloat16 [3, 3, 512, 512], replicated, may hold values from -0.09375 to 0.09375
- output_weight: bfloat16 [3, 3, 512, 512], replicated, may hold values from -0.09375 to 0.09375
- pole_index: int32 [512], replicated, may hold values from 0 to 15
- gelu_scale: float32 [512], replicated, may hold values from 0.15 to 0.6
- start_state: float32 [64, 128, 512], P('sx', 'sy'), may hold values from -12 to 12
Outputs:
- result: bfloat16 [32, 64, 128, 512], P('tm', 'sx', 'sy')
All inputs are finite; a program needn't handle non-finite values.
Results may differ from a plain program's by a relative error of at most 0.0049.
Values may be sent and summed in bfloat16 or wider, within the bound.
A program may use at most 128 MiB of HBM per device.

v0:
```python
import math

import jax
import jax.numpy as jnp
from jax import lax
from jax.sharding import PartitionSpec as P

NPOLES = 16


def extended(cells, sides, width):
    for axis, dim in sides:
        count = lax.axis_size(axis)
        ends = count - 1
        head = lax.slice_in_dim(cells, 0, width, axis=dim)
        tail = lax.slice_in_dim(cells, cells.shape[dim] - width, cells.shape[dim], axis=dim)
        cells = jnp.concatenate(
            [
                lax.ppermute(tail, axis, [(i, (i + 1) % count) for i in range(ends)]),
                cells,
                lax.ppermute(head, axis, [((i + 1) % count, i) for i in range(ends)]),
            ],
            axis=dim,
        )
    return cells


def carried_in(value, axis, join, neutral):
    count, mine = (lax.axis_size(axis), lax.axis_index(axis))
    pieces = jax.tree.map(lambda part: lax.all_gather(part, axis), value)
    so_far = jax.tree.map(
        lambda part, zero: jnp.full_like(part, 0) + jnp.asarray(zero, part.dtype), value, neutral
    )

    def lap(position, so_far):
        longer = join(so_far, jax.tree.map(lambda part: part[position], pieces))
        return jax.tree.map(lambda new, old: jnp.where(position < mine, new, old), longer, so_far)

    return lax.fori_loop(0, count - 1, lap, so_far)


def convolve_tile(padded, weight, rows, cols):
    count = padded.shape[0]
    channels = weight.shape[2]
    total = jnp.zeros((count * rows * cols, channels), jnp.float32)
    for row_shift in range(3):
        for col_shift in range(3):
            window = padded[
                :, row_shift : row_shift + rows, col_shift : col_shift + cols, :
            ].reshape(-1, channels)
            total = total + jnp.dot(
                window, weight[row_shift, col_shift], preferred_element_type=jnp.float32
            )
    return total.reshape(count, rows, cols, channels)


def combine(earlier, later):
    return (earlier[0] * later[0], later[0] * earlier[1] + later[1])


def on_device(frames, input_weight, output_weight, pole_index, gelu_scale, start_state):
    count, rows, cols, channels = frames.shape
    padded = extended(frames, (("sx", 1), ("sy", 2)), 1)
    drive = convolve_tile(padded, input_weight, rows, cols)
    decay = jnp.exp(
        -0.001 * jnp.exp(pole_index.astype(jnp.float32) * (math.log(300.0) / (NPOLES - 1)))
    )
    state = jnp.zeros(drive.shape[1:], jnp.float32)
    partial_states = []
    for step in range(count):
        state = decay * state + drive[step]
        partial_states.append(state)
    carried = decay**count
    identity = (jnp.ones_like(carried), jnp.zeros_like(state))
    prefix_decay, prefix_state = carried_in((carried, state), "tm", combine, identity)
    incoming = prefix_decay * start_state + prefix_state
    activated = []
    for step in range(count):
        full_state = decay ** (step + 1) * incoming + partial_states[step]
        activated.append(jax.nn.gelu(gelu_scale * full_state).astype(jnp.bfloat16))
    mixed = jnp.stack(activated, axis=0)
    padded_mixed = extended(mixed, (("sx", 1), ("sy", 2)), 1)
    return convolve_tile(padded_mixed, output_weight, rows, cols).astype(jnp.bfloat16)


def solution(mesh):
    return jax.shard_map(
        on_device,
        mesh=mesh,
        in_specs=(P("tm", "sx", "sy", None), P(), P(), P(), P(), P("sx", "sy", None)),
        out_specs=P("tm", "sx", "sy", None),
        check_vma=False,
    )
```

profile of v0, /device:TPU:32, one launch (start us, length us, event | category | flops | bytes accessed | tf_op | source)
XLA Modules:
  0.0 218.8 jit_solution(4450401698571554286)
XLA Ops:
  7.4 1.7 collective-permute-start
  10.5 2.1 fusion.51
  13.2 4.1 %collective-permute-start.2 = (bf16[2,34,1,512]{3,1,2,0:T(8,128)(2,1)S(1)}, bf16[2,34,1,512]{3,1,2,0:T(8,128)(2,1)S(1)}, u32[]{:S(2)}, u32[]{:S(2)}) collective-permute-start(bf16[2,34,1,512]{3,1,2,0:T(8,128)(2,1)S(1)} %copy.12), channel_id=1, source_target_pairs={{0,1},{1,2},{2,3},{3,4},{4,5},{5,6},{6,7},{8,9},{9,10},{10,11},{11... | collective-permute-start | bytes 208904 | tf_op jit(solution)/shard_map/ppermute | solution.py:19
  17.3 2.0 collective-permute-start.3
  20.9 3.6 %collective-permute-done.3 = bf16[2,34,1,512]{3,1,2,0:T(8,128)(2,1)S(1)} collective-permute-done((bf16[2,34,1,512]{3,1,2,0:T(8,128)(2,1)S(1)}, bf16[2,34,1,512]{3,1,2,0:T(8,128)(2,1)S(1)}, u32[]{:S(2)}, u32[]{:S(2)}) %collective-permute-start.3) | collective-permute-done | bytes 69664 | tf_op jit(solution)/shard_map/ppermute | solution.py:21
  24.6 3.2 %pad_maximum_fusion.6 = (bf16[2,32,16,512]{3,2,1,0:T(8,128)(2,1)S(1)}, bf16[2,32,16,512]{3,2,1,0:T(8,128)(2,1)S(1)}, bf16[2,32,16,512]{3,2,1,0:T(8,128)(2,1)S(1)...) fusion(bf16[2,34,1,512]{3,2,1,0:T(2,128)(2,1)S(1)} %copy.15, ...), kind=kLoop, calls=%fused_computation.47 | loop fusion | flops 12582912 | bytes 7544832 | tf_op jit(solution)/shard_map/concatenate | solution.py:17
  33.9 24.0 %all-gather.1 = f32[16,1,512]{2,1,0:T(1,128)S(1)} all-gather(f32[1,1,512]{2,1,0:T(1,128)S(1)} %bitcast.143), channel_id=2, replica_groups=mesh['tm'=16,'sx'=2,'sy'=8] {'tm'}, dimensions={0}, use_global_device_ids=true | all-gather | bytes 34816 | tf_op jit(solution)/shard_map/all_gather | solution.py:30
  57.9 94.7 %all-gather.4.cloned.1.call-done = f32[16,32,16,512]{3,2,1,0:T(8,128)} async-done(((f32[1,32,16,512]{3,2,1,0:T(8,128)}), f32[16,32,16,512]{3,2,1,0:T(8,128)}) %all-gather.4.cloned.1.call-update) | async-done | bytes 16777232 | tf_op jit(solution)/shard_map/all_gather | solution.py:30
  152.7 32.9 %while.16 = (s32[]{:T(128)}, f32[512]{0:T(512)S(1)}, f32[32,16,512]{2,1,0:T(8,128)S(1)}, s32[]{:T(128)}, f32[16,512]{1,0:T(8,128)S(1)}, /*index=5*/f32[16,32,16,512]{3,2,1,0:T(8,128)}, s32[]{:T(128)}, s32[]{:T(128)}) while((s32[]{:T(128)}, f32[512]{0:T(512)S(1)}, f32[32,16,512]{2,1,0:T(8,128)S(1)}, s32[]{:T(128)}, ...), condition=%wide.region_1.2_spmd.clone, body=%wide.region_0.1_spmd.clone.sunk | while | flops 1050116 | bytes 3158131 | solution.py:39
  152.7 2.1 fusion.108
  154.9 2.1 fusion.108
  157.1 2.1 fusion.108
  159.3 2.1 fusion.108
  161.5 2.1 fusion.108
  163.7 2.1 fusion.108
  165.9 2.1 fusion.108
  168.1 2.1 fusion.108
  170.2 2.1 fusion.108
  172.4 2.1 fusion.108
  174.6 2.1 fusion.108
  176.8 2.1 fusion.108
  179.0 2.1 fusion.108
  181.2 2.1 fusion.108
  183.4 2.1 fusion.108
  185.6 2.3 %fusion.80 = (bf16[1,32,16,512]{3,2,1,0:T(8,128)(2,1)S(1)}, bf16[1,32,16,512]{3,2,1,0:T(8,128)(2,1)S(1)}) fusion(f32[32,16,512]{2,1,0:T(8,128)S(1)} %bitcast.117, f32[32,16,512]{2,1,0:T(8,128)S(1)} %bitcast.119, f32[512]{0:T(512)S(1)} %get-tuple-element.186, f32[512]{0:T(512)S(1)} %get-tuple-element.187, f32[512]{0:T(512)S(1)} %get-tuple-element.185, ...), kind=kLoop, calls=%fused_computation.108 | loop fusion | flops 7602176 | bytes 5253120 | tf_op jit(solution)/shard_map/stack | solution.py:81
  187.9 1.6 collective-permute-start.4
  190.8 1.8 collective-permute-done.5
  192.8 3.7 %collective-permute-start.6 = (bf16[2,34,1,512]{3,2,1,0:T(2,128)(2,1)S(1)}, bf16[2,34,1,512]{3,2,1,0:T(2,128)(2,1)S(1)}, u32[]{:S(2)}, u32[]{:S(2)}) collective-permute-start(bf16[2,34,1,512]{3,2,1,0:T(2,128)(2,1)S(1)} %get-tuple-element.169), channel_id=1, source_target_pairs={{0,1},{1,2},{2,3},{3,4},{4,5},{5,6},{6,7},{8,9},{9,10},{10,11},{11... | collective-permute-start | bytes 208904 | tf_op jit(solution)/shard_map/ppermute | solution.py:19
  196.5 2.7 %collective-permute-start.7 = (bf16[2,34,1,512]{3,2,1,0:T(2,128)(2,1)S(1)}, bf16[2,34,1,512]{3,2,1,0:T(2,128)(2,1)S(1)}, u32[]{:S(2)}, u32[]{:S(2)}) collective-permute-start(bf16[2,34,1,512]{3,2,1,0:T(2,128)(2,1)S(1)} %get-tuple-element.168), channel_id=1, source_target_pairs={{1,0},{2,1},{3,2},{4,3},{5,4},{6,5},{7,6},{9,8},{10,9},{11,10},{12... | collective-permute-start | bytes 208904 | tf_op jit(solution)/shard_map/ppermute | solution.py:21
  199.5 1.7 fusion.25
  202.6 1.4 collective-permute-done.7
  209.5 2.5 %add_convert_fusion = bf16[1024,512]{1,0:T(8,128)(2,1)} fusion(f32[1024,512]{1,0:T(8,128)S(1)} %fusion.25, f32[1024,512]{1,0:T(8,128)S(1)} %fusion.27, f32[1024,512]{1,0:T(8,128)S(1)} %fusion.29, f32[1024,512]{1,0:T(8,128)S(1)} %fusion.31, f32[1024,512]{1,0:T(8,128)S(1)} %fusion.33, f32[1024,512]{1,0:T(8,128)S(1)} %fusion.35, f32[1024,512]{1,0:T(8,128)S(1)} %fusion.39, ...), kind=kOutput, calls=%fused_computation.8 | convolution fusion | flops 541589504 | bytes 19398656 | tf_op jit(solution)/shard_map/dot_general | solution.py:51
  (87 shorter events, 19.5 us)
Async XLA Ops:
  6.5 6.1 %copy-start.1 = (bf16[2,32,16,512]{3,2,1,0:T(8,128)(2,1)S(1)}, bf16[2,32,16,512]{3,2,1,0:T(8,128)(2,1)}, u32[]{:S(2)}) copy-start(bf16[2,32,16,512]{3,2,1,0:T(8,128)(2,1)} %param.8) | copy-start | bytes 3145732
  6.5 6.0 %copy-start.3 = (s32[512]{0:T(512)S(1)}, s32[512]{0:T(512)}, u32[]{:S(2)}) copy-start(s32[512]{0:T(512)} %param.11) | copy-start | bytes 6148
  6.5 146.1 %all-gather.4.cloned.1.call-start = ((), (), s32[]{:S(2)}) async-start(), calls=%async_computation | async-start | bytes 17825792 | tf_op jit(solution)/shard_map/all_gather | solution.py:30
  7.4 5.1 %collective-permute-start = (bf16[2,1,16,512]{3,2,1,0:T(8,128)(2,1)S(1)}, bf16[2,1,16,512]{3,2,1,0:T(8,128)(2,1)S(1)}, u32[]{:S(2)}, u32[]{:S(2)}) collective-permute-start(bf16[2,1,16,512]{3,2,1,0:T(8,128)(2,1)S(1)} %get-tuple-element.183), channel_id=1, source_target_pairs={{0,8},{1,9},{2,10},{3,11},{4,12},{5,13},{6,14},{7,15},{16,24},{17,... | collective-permute-start | bytes 98312 | tf_op jit(solution)/shard_map/ppermute | solution.py:19
  9.2 3.4 %collective-permute-start.1 = (bf16[2,1,16,512]{3,2,1,0:T(8,128)(2,1)S(1)}, bf16[2,1,16,512]{3,2,1,0:T(8,128)(2,1)S(1)}, u32[]{:S(2)}, u32[]{:S(2)}) collective-permute-start(bf16[2,1,16,512]{3,2,1,0:T(8,128)(2,1)S(1)} %get-tuple-element.184), channel_id=1, source_target_pairs={{8,0},{9,1},{10,2},{11,3},{12,4},{13,5},{14,6},{15,7},{24,16},{25,... | collective-permute-start | bytes 98312 | tf_op jit(solution)/shard_map/ppermute | solution.py:21
  12.6 6.8 %copy-start = (bf16[3,3,512,512]{3,2,1,0:T(8,128)(2,1)S(1)}, bf16[3,3,512,512]{3,2,1,0:T(8,128)(2,1)}, u32[]{:S(2)}) copy-start(bf16[3,3,512,512]{3,2,1,0:T(8,128)(2,1)} %param.9) | copy-start | bytes 14155780
  13.2 7.6 %collective-permute-start.2 = (bf16[2,34,1,512]{3,1,2,0:T(8,128)(2,1)S(1)}, bf16[2,34,1,512]{3,1,2,0:T(8,128)(2,1)S(1)}, u32[]{:S(2)}, u32[]{:S(2)}) collective-permute-start(bf16[2,34,1,512]{3,1,2,0:T(8,128)(2,1)S(1)} %copy.12), channel_id=1, source_target_pairs={{0,1},{1,2},{2,3},{3,4},{4,5},{5,6},{6,7},{8,9},{9,10},{10,11},{11... | collective-permute-start | bytes 208904 | tf_op jit(solution)/shard_map/ppermute | solution.py:19
  17.3 7.2 %collective-permute-start.3 = (bf16[2,34,1,512]{3,1,2,0:T(8,128)(2,1)S(1)}, bf16[2,34,1,512]{3,1,2,0:T(8,128)(2,1)S(1)}, u32[]{:S(2)}, u32[]{:S(2)}) collective-permute-start(bf16[2,34,1,512]{3,1,2,0:T(8,128)(2,1)S(1)} %copy.14), channel_id=1, source_target_pairs={{1,0},{2,1},{3,2},{4,3},{5,4},{6,5},{7,6},{9,8},{10,9},{11,10},{12... | collective-permute-start | bytes 208904 | tf_op jit(solution)/shard_map/ppermute | solution.py:21
  152.7 32.9 %copy-start.2 = (f32[512]{0:T(512)S(1)}, f32[512]{0:T(512)}, u32[]{:S(2)}) copy-start(f32[512]{0:T(512)} %param.12) | copy-start | bytes 6148
  187.9 2.9 %collective-permute-start.4 = (bf16[2,1,16,512]{3,2,1,0:T(8,128)(2,1)S(1)}, bf16[2,1,16,512]{3,2,1,0:T(8,128)(2,1)S(1)}, u32[]{:S(2)}, u32[]{:S(2)}) collective-permute-start(bf16[2,1,16,512]{3,2,1,0:T(8,128)(2,1)S(1)} %get-tuple-element.178), channel_id=1, source_target_pairs={{0,8},{1,9},{2,10},{3,11},{4,12},{5,13},{6,14},{7,15},{16,24},{17,... | collective-permute-start | bytes 98312 | tf_op jit(solution)/shard_map/ppermute | solution.py:19
  189.5 3.1 %collective-permute-start.5 = (bf16[2,1,16,512]{3,2,1,0:T(8,128)(2,1)S(1)}, bf16[2,1,16,512]{3,2,1,0:T(8,128)(2,1)S(1)}, u32[]{:S(2)}, u32[]{:S(2)}) collective-permute-start(bf16[2,1,16,512]{3,2,1,0:T(8,128)(2,1)S(1)} %get-tuple-element.179), channel_id=1, source_target_pairs={{8,0},{9,1},{10,2},{11,3},{12,4},{13,5},{14,6},{15,7},{24,16},{25,... | collective-permute-start | bytes 98312 | tf_op jit(solution)/shard_map/ppermute | solution.py:21
  192.6 8.6 %slice-start = ((s8[4718592]{0:T(1024)(128)(4,1)}), s8[4194304]{0:T(1024)(128)(4,1)S(1)}, s32[]{:S(2)}) async-start(s8[4718592]{0:T(1024)(128)(4,1)} %bitcast.120), calls=%async_computation.1 | async-start | bytes 8388608
  192.8 9.9 %collective-permute-start.6 = (bf16[2,34,1,512]{3,2,1,0:T(2,128)(2,1)S(1)}, bf16[2,34,1,512]{3,2,1,0:T(2,128)(2,1)S(1)}, u32[]{:S(2)}, u32[]{:S(2)}) collective-permute-start(bf16[2,34,1,512]{3,2,1,0:T(2,128)(2,1)S(1)} %get-tuple-element.169), channel_id=1, source_target_pairs={{0,1},{1,2},{2,3},{3,4},{4,5},{5,6},{6,7},{8,9},{9,10},{10,11},{11... | collective-permute-start | bytes 208904 | tf_op jit(solution)/shard_map/ppermute | solution.py:19
  196.5 4.7 %slice-start.1 = ((s8[4718592]{0:T(1024)(128)(4,1)}), s8[524288]{0:T(1024)(128)(4,1)S(1)}, s32[]{:S(2)}) async-start(s8[4718592]{0:T(1024)(128)(4,1)} %bitcast.120), calls=%async_computation.2 | async-start | bytes 1048576
  196.5 7.5 %collective-permute-start.7 = (bf16[2,34,1,512]{3,2,1,0:T(2,128)(2,1)S(1)}, bf16[2,34,1,512]{3,2,1,0:T(2,128)(2,1)S(1)}, u32[]{:S(2)}, u32[]{:S(2)}) collective-permute-start(bf16[2,34,1,512]{3,2,1,0:T(2,128)(2,1)S(1)} %get-tuple-element.168), channel_id=1, source_target_pairs={{1,0},{2,1},{3,2},{4,3},{5,4},{6,5},{7,6},{9,8},{10,9},{11,10},{12... | collective-permute-start | bytes 208904 | tf_op jit(solution)/shard_map/ppermute | solution.py:21
Sparse Core Ops, SparseCore 0:
  34.0 118.6 all-gather.3
where the time goes:
time: 221 us; the launch traced here: 219 us
  waiting for transfers between devices  102 us (46%)
  other arithmetic  40.8 us (18%)
  blocking collectives  24 us (11%)
  starting transfers between devices  18.4 us (8%)
  matrix products  17.3 us (8%)
  between operations  13.8 us (6%)
  local copies, waits for them, and re-layouts  2.57 us (1%)
    all_gather x1, waiting for transfers between devices, carried_in(): pieces = jax.tree.map(lambda part: lax.all_gather(part, axis), value)  94.7 us
    select_n x30, other arithmetic, lap(): jnp.where(position < mine, new, old)  32.3 us
    all_gather x1, blocking collectives, carried_in(): pieces = jax.tree.map(lambda part: lax.all_gather(part, axis), value)  24 us
    dot_general x18, matrix products, convolve_tile(): jnp.dot(window, weight[row_shift, col_shift], preferred_element_type=jnp....  17.3 us
    ppermute x4, starting transfers between devices, extended(): lax.ppermute(tail, axis, [(i, (i + 1) % count) for i in range(ends)])  11.1 us
    ppermute x4, starting transfers between devices, extended(): lax.ppermute(head, axis, [((i + 1) % count, i) for i in range(ends)])  7.29 us
    ppermute x4, waiting for transfers between devices, extended(): lax.ppermute(head, axis, [((i + 1) % count, i) for i in range(ends)])  6.74 us
    concatenate x5, other arithmetic, extended(): jnp.concatenate([lax.ppermute(tail, axis, [(i, (i + 1) % count) for i in...  5 us
  transfers between devices with their start and end apart: 9, of which 4 were waited for; matrix products, arithmetic and copies ran while one was open for 3% of the time, Pallas kernels for 0%

commit v1 on v0

v1 whole, which is shorter than its diff:
```python
import functools
import math

import jax
import jax.numpy as jnp
from jax import lax
from jax.experimental import pallas as pl
from jax.experimental.pallas import tpu as pltpu
from jax.sharding import PartitionSpec as P

NPOLES = 16
CHUNKS = 4
MESH = pl.DeviceIdType.MESH
F32 = jnp.float32
BF16 = jnp.bfloat16


def layer_kernel(
    sizes,
    frames_hbm, w1_hbm, w2_hbm, pole_ref, scale_ref, start_hbm, out_hbm,
    raw, wide, xf, xm, drive, w1, w2, ends, gathered, prefixes, carried, first, out,
    decay_ref, decay2_ref, edge_out, edge_in, side_out, side_in,
    frame_sem, w1_sem, w2_sem, first_sem, out_sem,
    col_send, col_recv, row_send, row_recv,
    end_send, end_recv, pre_send, pre_recv,
):
    peers, zs, rows, cols, ch = sizes
    n = CHUNKS
    step = rows // n
    split = peers // step
    lanes = ch // split
    me, sx, z = lax.axis_index("tm"), lax.axis_index("sx"), lax.axis_index("sy")
    other = 1 - sx
    right, left = lax.rem(z + 1, zs), lax.rem(z + zs - 1, zs)
    piece_row, piece_part = me // split, lax.rem(me, split)

    def row_of(lo, hi):
        return jnp.where(sx == 0, rows - hi, lo)

    def base(c):
        return row_of(c * step, (c + 1) * step)

    border = jnp.where(sx == 0, rows, 1)
    blank = jnp.where(sx == 0, 0, rows + 1)
    halo_there = jnp.where(sx == 0, 0, rows + 1)

    frame_copy = pltpu.make_async_copy(frames_hbm, raw, frame_sem)
    frame_copy.start()
    w1_copies = [pltpu.make_async_copy(w1_hbm.at[i], w1.at[i], w1_sem.at[i]) for i in range(3)]
    for copy in w1_copies:
        copy.start()

    barrier = pltpu.get_barrier_semaphore()
    for k in range(1, peers):
        pl.semaphore_signal(barrier, inc=1, device_id={"tm": lax.rem(me + k, peers)}, device_id_type=MESH)
    for where in ({"sy": left}, {"sy": right}, {"sx": other}):
        pl.semaphore_signal(barrier, inc=1, device_id=where, device_id_type=MESH)

    first_copies = []
    for c in range(n):
        copy = pltpu.make_async_copy(
            start_hbm.at[base(c) + piece_row, :, pl.ds(pl.multiple_of(piece_part * lanes, lanes), lanes)],
            first.at[c], first_sem.at[c],
        )
        copy.start()
        first_copies.append(copy)
    w2_copies = [pltpu.make_async_copy(w2_hbm.at[i], w2.at[i], w2_sem.at[i]) for i in range(3)]
    for copy in w2_copies:
        copy.start()

    decay = jnp.exp(-0.001 * jnp.exp(pole_ref[...].astype(F32) * (math.log(300.0) / (NPOLES - 1))))
    decay_ref[...] = decay
    for part in range(split):
        decay2_ref[part] = (decay * decay)[:, part * lanes : (part + 1) * lanes]
    for padded in (xf, xm):
        padded[:, pl.ds(blank, 1)] = jnp.zeros((2, 1, cols, 3 * ch), BF16)

    def side_refs(slot):
        return (edge_out, edge_in) if slot == n else (side_out.at[slot], side_in.at[slot])

    def side_copies(slot):
        src, dst = side_refs(slot)
        return [
            pltpu.make_async_remote_copy(
                src.at[d], dst.at[d], col_send.at[slot, d], col_recv.at[slot, d],
                device_id={"sy": to}, device_id_type=MESH,
            )
            for d, to in ((0, right), (1, left))
        ]

    def row_copy(padded, slot):
        return pltpu.make_async_remote_copy(
            padded.at[:, pl.ds(border, 1)], padded.at[:, pl.ds(halo_there, 1)],
            row_send.at[slot], row_recv.at[slot],
            device_id={"sx": other}, device_id_type=MESH,
        )

    def send_sides(slot, at, count):
        src = side_refs(slot)[0]
        for f in range(2):
            spot = pl.ds(f * rows + at, count)
            last, head = wide[spot, 7 + cols, :], wide[spot, 8, :]
            src[0, f] = last.astype(BF16)
            src[1, f] = head.astype(BF16)
        copies = side_copies(slot)
        for copy in copies:
            copy.start()
        return copies

    def place_sides(slot, at, count):
        dst = side_refs(slot)[1]
        for f in range(2):
            spot = pl.ds(f * rows + at, count)
            for d, col, kept in ((0, 7, z > 0), (1, 8 + cols, z < zs - 1)):
                wide[spot, col, :] = jnp.where(kept, dst[d, f].astype(F32), 0.0)

    def spread(padded, at, count):
        for f in range(2):
            for r in range(count):
                for j in range(3):
                    padded[f, at + r + 1, :, j * ch : (j + 1) * ch] = wide[f * rows + at + r, 7 + j : 7 + j + cols, :].astype(BF16)

    def conv(padded, weight, at, count):
        window = jnp.concatenate(
            [padded[:, pl.ds(at + i, count)].reshape(2 * count * cols, 3 * ch) for i in range(3)], axis=-1
        )
        return jnp.dot(window, weight[...].reshape(9 * ch, ch), preferred_element_type=F32).reshape(2, count, cols, ch)

    frame_copy.wait()

    def widen(r, _):
        for f in range(2):
            wide[f * rows + r, 8 : 8 + cols, :] = raw[f, r].astype(F32)
        return 0

    lax.fori_loop(0, rows, widen, 0, unroll=4)
    pl.semaphore_wait(barrier, peers + 2)
    waits = send_sides(n, 0, rows)
    for copy in waits:
        copy.wait_recv()
    place_sides(n, 0, rows)
    spread(xf, base(0), step)
    row_f = row_copy(xf, 0)
    row_f.start()
    sent = [copy.wait_send for copy in waits] + [row_f.wait_send]

    def rest(c, _):
        spread(xf, base(c), step)
        return 0

    lax.fori_loop(1, n, rest, 0)
    row_f.wait_recv()
    for copy in w1_copies:
        copy.wait()

    def all_of(ref, sem):
        return pltpu.make_async_copy(ref, ref, sem)

    def exchange(src, dst, send, recv, c):
        pltpu.make_async_copy(src.at[c, me], dst.at[c, me], recv.at[c]).start()
        for k in range(1, peers):
            to = lax.rem(me + k, peers)
            pltpu.make_async_remote_copy(
                src.at[c, to], dst.at[c, me], send.at[c], recv.at[c],
                device_id={"tm": to}, device_id_type=MESH,
            ).start()
        sent.append(all_of(src.at[c, pl.ds(0, peers - 1)], send.at[c]).wait)

    def drive_chunk(c):
        got = conv(xf, w1, base(c), step)
        drive[c] = got
        end = decay_ref[...].reshape(1, 1, ch) * got[0] + got[1]
        for r in range(step):
            for part in range(split):
                ends[c, r * split + part] = end[r, :, part * lanes : (part + 1) * lanes].astype(BF16)
        exchange(ends, gathered, end_send, end_recv, c)

    def prefix_chunk(c):
        first_copies[c].wait()
        all_of(gathered.at[c], end_recv.at[c]).wait()
        square = decay2_ref[pl.ds(piece_part, 1)].reshape(1, lanes)
        state = first[c]
        for i in range(peers):
            prefixes[c, i] = state.astype(BF16)
            if i < peers - 1:
                state = square * state + gathered[c, i].astype(F32)
        exchange(prefixes, carried, pre_send, pre_recv, c)

    def mix_chunk(c):
        all_of(carried.at[c], pre_recv.at[c]).wait()
        at = base(c)
        for r in range(step):
            state = jnp.concatenate([carried[c, r * split + part] for part in range(split)], axis=-1).astype(F32)
            for f in range(2):
                state = decay_ref[...] * state + drive[c, f, r]
                wide[f * rows + at + r, 8 : 8 + cols, :] = jax.nn.gelu(scale_ref[...] * state)
        return send_sides(c, at, step)

    row_m = row_copy(xm, 1)

    def lay_chunk(c, copies):
        at = base(c)
        for copy in copies:
            copy.wait_recv()
            sent.append(copy.wait_send)
        place_sides(c, at, step)
        spread(xm, at, step)
        if c == 0:
            row_m.start()
            sent.append(row_m.wait_send)

    def result_chunk(c):
        lo = max(c * step - 1, 0)
        hi = rows if c == n - 1 else (c + 1) * step - 1
        at = row_of(lo, hi)
        if c == 0:
            row_m.wait_recv()
            for copy in w2_copies:
                copy.wait()
        out[:, pl.ds(at, hi - lo)] = conv(xm, w2, at, hi - lo).astype(BF16)
        copy = pltpu.make_async_copy(out.at[:, pl.ds(at, hi - lo)], out_hbm.at[:, pl.ds(at, hi - lo)], out_sem.at[c])
        copy.start()
        sent.append(copy.wait)

    for c in range(n):
        drive_chunk(c)
        if c >= 2:
            prefix_chunk(c - 2)
    sides = {}
    for c in range(max(n - 2, 0), n):
        prefix_chunk(c)
    for c in range(n):
        sides[c] = mix_chunk(c)
        if c >= 1:
            lay_chunk(c - 1, sides[c - 1])
            result_chunk(c - 1)
    lay_chunk(n - 1, sides[n - 1])
    result_chunk(n - 1)
    for wait in sent:
        wait()


def on_device(peers, zs, frames, input_weight, output_weight, pole_index, gelu_scale, start_state):
    count, rows, cols, ch = frames.shape
    n = CHUNKS
    step = rows // n
    split = peers // step
    lanes = ch // split
    any_space = pl.BlockSpec(memory_space=pl.ANY)
    vmem = pl.BlockSpec(memory_space=pltpu.VMEM)
    dma = pltpu.SemaphoreType.DMA
    pieces = pltpu.VMEM((n, peers, cols, lanes), BF16)
    return pl.pallas_call(
        functools.partial(layer_kernel, (peers, zs, rows, cols, ch)),
        out_shape=jax.ShapeDtypeStruct(frames.shape, BF16),
        in_specs=[any_space, any_space, any_space, vmem, vmem, any_space],
        out_specs=any_space,
        scratch_shapes=[
            pltpu.VMEM((count, rows, cols, ch), BF16),
            pltpu.VMEM((count * rows, 32, ch), F32),
            pltpu.VMEM((count, rows + 2, cols, 3 * ch), BF16),
            pltpu.VMEM((count, rows + 2, cols, 3 * ch), BF16),
            pltpu.VMEM((n, count, step, cols, ch), F32),
            pltpu.VMEM((3, 3 * ch, ch), BF16),
            pltpu.VMEM((3, 3 * ch, ch), BF16),
            pieces, pieces, pieces, pieces,
            pltpu.VMEM((n, cols, lanes), F32),
            pltpu.VMEM((count, rows, cols, ch), BF16),
            pltpu.VMEM((1, ch), F32),
            pltpu.VMEM((split, 1, lanes), F32),
            pltpu.VMEM((2, count, rows, ch), BF16),
            pltpu.VMEM((2, count, rows, ch), BF16),
            pltpu.VMEM((n, 2, count, step, ch), BF16),
            pltpu.VMEM((n, 2, count, step, ch), BF16),
            dma, dma((3,)), dma((3,)), dma((n,)), dma((n,)),
            dma((n + 1, 2)), dma((n + 1, 2)), dma((2,)), dma((2,)),
            dma((n,)), dma((n,)), dma((n,)), dma((n,)),
        ],
        compiler_params=pltpu.CompilerParams(
            collective_id=0, has_side_effects=True, vmem_limit_bytes=56 << 20
        ),
        name="layer",
    )(
        frames,
        input_weight.reshape(3, 3 * ch, ch),
        output_weight.reshape(3, 3 * ch, ch),
        pole_index.reshape(1, ch),
        gelu_scale.reshape(1, ch),
        start_state,
    )


def solution(mesh):
    return jax.shard_map(
        functools.partial(on_device, mesh.shape["tm"], mesh.shape["sy"]),
        mesh=mesh,
        in_specs=(P("tm", "sx", "sy", None), P(), P(), P(), P(), P("sx", "sy", None)),
        out_specs=P("tm", "sx", "sy", None),
        check_vma=False,
    )
```

time: 221 us -> 46.7 us (0.21)
  the two profiles are of different devices: /device:TPU:32 before, /device:TPU:1 now
where the time goes in v1:
time: 46.7 us; the launch traced here: 46.6 us
  Pallas kernels  44.3 us (95%)
  local copies, waits for them, and re-layouts  2.26 us (5%)
    pallas_call x1, Pallas kernels, on_device(): pl.pallas_call(functools.partial(layer_kernel, (peers, zs, rows, cols, ch...  44.3 us
    unnamed x1, local copies, waits for them, and re-layouts  2.26 us

profile of v1, /device:TPU:1, one launch (start us, length us, event | category | flops | bytes accessed | tf_op | source)
XLA Modules:
  0.0 46.6 jit_solution(2822487794869748558)
XLA Ops:
  0.0 44.3 %layer.1 = bf16[2,32,16,512]{3,2,1,0:T(8,128)(2,1)} custom-call(bf16[2,32,16,512]{3,2,1,0:T(8,128)(2,1)} %frames_hbm.1, bf16[3,1536,512]{2,1,0:T(8,128)(2,1)} %bitcast.4, bf16[3,1536,512]{2,1,0:T(8,128)(2,1)} %bitcast.5, s32[1,512]{1,0:T(1,128)} %bitcast.6, f32[1,512]{1,0:T(1,128)} %bitcast.7, f32[32,16,512]{2,1,0:T(8,128)} %start_hbm.1), custom_call_target="tpu_custom_call" | custom-call | tf_op jit(solution)/shard_map/layer/pallas_call | solution.py:253
  44.3 2.3 %copy.8 = bf16[2,32,16,512]{3,2,1,0:T(8,128)(2,1)} copy(bf16[2,32,16,512]{3,2,1,0:T(8,128)(2,1)} %layer.1) | data formatting | bytes 2097152

commit v2 on v1

--- a/solution.py
+++ b/solution.py
@@ -17,14 +17,15 @@
 
 def layer_kernel(
     sizes,
-    frames_hbm, w1_hbm, w2_hbm, pole_ref, scale_ref, start_hbm, out_hbm,
-    raw, wide, xf, xm, drive, w1, w2, ends, gathered, prefixes, carried, first, out,
+    frames_hbm, w1_hbm, w2_hbm, pole_hbm, scale_hbm, start_hbm, out,
+    wide, xf, xm, drive, w1, w2, ends, gathered, prefixes, carried, first, pole_ref, scale_ref,
     decay_ref, decay2_ref, edge_out, edge_in, side_out, side_in,
-    frame_sem, w1_sem, w2_sem, first_sem, out_sem,
+    frame_sem, small_sem, w1_sem, w2_sem, first_sem, near_sem,
     col_send, col_recv, row_send, row_recv,
     end_send, end_recv, pre_send, pre_recv,
 ):
     peers, zs, rows, cols, ch = sizes
+    side = math.isqrt(peers)
     n = CHUNKS
     step = rows // n
     split = peers // step
@@ -44,17 +45,43 @@
     blank = jnp.where(sx == 0, 0, rows + 1)
     halo_there = jnp.where(sx == 0, 0, rows + 1)
 
-    frame_copy = pltpu.make_async_copy(frames_hbm, raw, frame_sem)
+    mid = pl.ds(ch, ch)
+    frame_copy = pltpu.make_async_copy(frames_hbm, xf.at[:, pl.ds(1, rows), :, mid], frame_sem)
     frame_copy.start()
-    w1_copies = [pltpu.make_async_copy(w1_hbm.at[i], w1.at[i], w1_sem.at[i]) for i in range(3)]
-    for copy in w1_copies:
+
+    def weight_copies(src, dst, sems):
+        return [
+            pltpu.make_async_copy(src.at[:, pl.ds(j * ch, ch)], dst.at[:, pl.ds(j * ch, ch)], sems.at[j])
+            for j in range(3)
+        ]
+
+    small_copies = [
+        pltpu.make_async_copy(pole_hbm, pole_ref, small_sem.at[0]),
+        pltpu.make_async_copy(scale_hbm, scale_ref, small_sem.at[1]),
+    ]
+    for copy in small_copies:
         copy.start()
-
+    w1_copies = weight_copies(w1_hbm, w1, w1_sem)
+    for j in (1, 0, 2):
+        w1_copies[j].start()
+
+    y, x = me // side, lax.rem(me, side)
+    around = [
+        {"tm": y * side + lax.rem(x + 1, side)},
+        {"tm": y * side + lax.rem(x + side - 1, side)},
+        {"tm": lax.rem(y + 1, side) * side + x},
+        {"tm": lax.rem(y + side - 1, side) * side + x},
+    ]
     barrier = pltpu.get_barrier_semaphore()
-    for k in range(1, peers):
-        pl.semaphore_signal(barrier, inc=1, device_id={"tm": lax.rem(me + k, peers)}, device_id_type=MESH)
-    for where in ({"sy": left}, {"sy": right}, {"sx": other}):
+    for where in [{"sy": left}, {"sy": right}, {"sx": other}] + around:
         pl.semaphore_signal(barrier, inc=1, device_id=where, device_id_type=MESH)
+
+    def tell(k):
+        for where in around:
+            pl.semaphore_signal(near_sem.at[k], inc=1, device_id=where, device_id_type=MESH)
+
+    def hear(k):
+        pl.semaphore_wait(near_sem.at[k], len(around))
 
     first_copies = []
     for c in range(n):
@@ -64,14 +91,10 @@
         )
         copy.start()
         first_copies.append(copy)
-    w2_copies = [pltpu.make_async_copy(w2_hbm.at[i], w2.at[i], w2_sem.at[i]) for i in range(3)]
+    w2_copies = weight_copies(w2_hbm, w2, w2_sem)
     for copy in w2_copies:
         copy.start()
 
-    decay = jnp.exp(-0.001 * jnp.exp(pole_ref[...].astype(F32) * (math.log(300.0) / (NPOLES - 1))))
-    decay_ref[...] = decay
-    for part in range(split):
-        decay2_ref[part] = (decay * decay)[:, part * lanes : (part + 1) * lanes]
     for padded in (xf, xm):
         padded[:, pl.ds(blank, 1)] = jnp.zeros((2, 1, cols, 3 * ch), BF16)
 
@@ -102,6 +125,9 @@
             last, head = wide[spot, 7 + cols, :], wide[spot, 8, :]
             src[0, f] = last.astype(BF16)
             src[1, f] = head.astype(BF16)
+        if slot == n:
+            pl.semaphore_wait(barrier, 3 + len(around))
+            tell(0)
         copies = side_copies(slot)
         for copy in copies:
             copy.start()
@@ -117,41 +143,58 @@
     def spread(padded, at, count):
         for f in range(2):
             for r in range(count):
-                for j in range(3):
+                for j in (0, 2):
                     padded[f, at + r + 1, :, j * ch : (j + 1) * ch] = wide[f * rows + at + r, 7 + j : 7 + j + cols, :].astype(BF16)
 
-    def conv(padded, weight, at, count):
-        window = jnp.concatenate(
-            [padded[:, pl.ds(at + i, count)].reshape(2 * count * cols, 3 * ch) for i in range(3)], axis=-1
+    def dots(padded, weight, at, count, js):
+        left_side = jnp.concatenate(
+            [
+                padded[:, pl.ds(at + i, count), :, j * ch : (j + 1) * ch].reshape(2 * count * cols, ch)
+                for i in range(3) for j in js
+            ],
+            axis=-1,
         )
-        return jnp.dot(window, weight[...].reshape(9 * ch, ch), preferred_element_type=F32).reshape(2, count, cols, ch)
+        right_side = jnp.concatenate([weight[i, j * ch : (j + 1) * ch] for i in range(3) for j in js], axis=0)
+        return jnp.dot(left_side, right_side, preferred_element_type=F32).reshape(2, count, cols, ch)
 
     frame_copy.wait()
 
     def widen(r, _):
         for f in range(2):
-            wide[f * rows + r, 8 : 8 + cols, :] = raw[f, r].astype(F32)
+            wide[f * rows + r, 8 : 8 + cols, :] = xf[f, r + 1, :, ch : 2 * ch].astype(F32)
         return 0
 
     lax.fori_loop(0, rows, widen, 0, unroll=4)
-    pl.semaphore_wait(barrier, peers + 2)
-    waits = send_sides(n, 0, rows)
-    for copy in waits:
+    edges = send_sides(n, 0, rows)
+    for copy in small_copies:
+        copy.wait()
+    decay = jnp.exp(-0.001 * jnp.exp(pole_ref[...].astype(F32) * (math.log(300.0) / (NPOLES - 1))))
+    decay_ref[...] = decay
+    for part in range(split):
+        decay2_ref[part] = (decay * decay)[:, part * lanes : (part + 1) * lanes]
+    w1_copies[1].wait()
+    drive[1] = dots(xf, w1, base(1), step, (1,))
+    hear(0)
+    tell(1)
+    for c in range(2, n - 1):
+        drive[c] = dots(xf, w1, base(c), step, (1,))
+    hear(1)
+    tell(2)
+    for copy in edges:
         copy.wait_recv()
     place_sides(n, 0, rows)
     spread(xf, base(0), step)
     row_f = row_copy(xf, 0)
     row_f.start()
-    sent = [copy.wait_send for copy in waits] + [row_f.wait_send]
+    sent = [copy.wait_send for copy in edges] + [row_f.wait_send]
 
     def rest(c, _):
         spread(xf, base(c), step)
         return 0
 
     lax.fori_loop(1, n, rest, 0)
-    row_f.wait_recv()
-    for copy in w1_copies:
-        copy.wait()
+    w1_copies[0].wait()
+    w1_copies[2].wait()
 
     def all_of(ref, sem):
         return pltpu.make_async_copy(ref, ref, sem)
@@ -167,12 +210,19 @@
         sent.append(all_of(src.at[c, pl.ds(0, peers - 1)], send.at[c]).wait)
 
     def drive_chunk(c):
-        got = conv(xf, w1, base(c), step)
+        if c == 0:
+            row_f.wait_recv()
+        if 1 <= c < n - 1:
+            got = drive[c] + dots(xf, w1, base(c), step, (0, 2))
+        else:
+            got = dots(xf, w1, base(c), step, (0, 1, 2))
         drive[c] = got
         end = decay_ref[...].reshape(1, 1, ch) * got[0] + got[1]
         for r in range(step):
             for part in range(split):
                 ends[c, r * split + part] = end[r, :, part * lanes : (part + 1) * lanes].astype(BF16)
+        if c == 1:
+            hear(2)
         exchange(ends, gathered, end_send, end_recv, c)
 
     def prefix_chunk(c):
@@ -193,14 +243,17 @@
             state = jnp.concatenate([carried[c, r * split + part] for part in range(split)], axis=-1).astype(F32)
             for f in range(2):
                 state = decay_ref[...] * state + drive[c, f, r]
-                wide[f * rows + at + r, 8 : 8 + cols, :] = jax.nn.gelu(scale_ref[...] * state)
-        return send_sides(c, at, step)
-
+                mixed = jax.nn.gelu(scale_ref[...] * state)
+                wide[f * rows + at + r, 8 : 8 + cols, :] = mixed
+                xm[f, at + r + 1, :, ch : 2 * ch] = mixed.astype(BF16)
+        sides[c] = send_sides(c, at, step)
+
+    sides = {}
     row_m = row_copy(xm, 1)
 
-    def lay_chunk(c, copies):
+    def lay_chunk(c):
         at = base(c)
-        for copy in copies:
+        for copy in sides[c]:
             copy.wait_recv()
             sent.append(copy.wait_send)
         place_sides(c, at, step)
@@ -213,29 +266,36 @@
         lo = max(c * step - 1, 0)
         hi = rows if c == n - 1 else (c + 1) * step - 1
         at = row_of(lo, hi)
-        if c == 0:
-            row_m.wait_recv()
-            for copy in w2_copies:
-                copy.wait()
-        out[:, pl.ds(at, hi - lo)] = conv(xm, w2, at, hi - lo).astype(BF16)
-        copy = pltpu.make_async_copy(out.at[:, pl.ds(at, hi - lo)], out_hbm.at[:, pl.ds(at, hi - lo)], out_sem.at[c])
-        copy.start()
-        sent.append(copy.wait)
-
-    for c in range(n):
-        drive_chunk(c)
-        if c >= 2:
-            prefix_chunk(c - 2)
-    sides = {}
-    for c in range(max(n - 2, 0), n):
-        prefix_chunk(c)
-    for c in range(n):
-        sides[c] = mix_chunk(c)
-        if c >= 1:
-            lay_chunk(c - 1, sides[c - 1])
-            result_chunk(c - 1)
-    lay_chunk(n - 1, sides[n - 1])
-    result_chunk(n - 1)
+        if c == n - 1:
+            part = dots(xm, w2, at, hi - lo, (1,))
+            lay_chunk(c)
+            got = part + dots(xm, w2, at, hi - lo, (0, 2))
+        else:
+            got = dots(xm, w2, at, hi - lo, (0, 1, 2))
+        out[:, pl.ds(at, hi - lo)] = got.astype(BF16)
+
+    drive_chunk(1)
+    drive_chunk(0)
+    drive_chunk(2)
+    prefix_chunk(1)
+    drive_chunk(3)
+    prefix_chunk(0)
+    prefix_chunk(2)
+    mix_chunk(1)
+    prefix_chunk(3)
+    mix_chunk(0)
+    for copy in w2_copies:
+        copy.wait()
+    lay_chunk(1)
+    lay_chunk(0)
+    mix_chunk(2)
+    result_chunk(1)
+    row_m.wait_recv()
+    result_chunk(0)
+    lay_chunk(2)
+    mix_chunk(3)
+    result_chunk(2)
+    result_chunk(3)
     for wait in sent:
         wait()
 
@@ -246,17 +306,16 @@
     step = rows // n
     split = peers // step
     lanes = ch // split
-    any_space = pl.BlockSpec(memory_space=pl.ANY)
+    in_hbm = pl.BlockSpec(memory_space=pltpu.HBM)
     vmem = pl.BlockSpec(memory_space=pltpu.VMEM)
     dma = pltpu.SemaphoreType.DMA
     pieces = pltpu.VMEM((n, peers, cols, lanes), BF16)
     return pl.pallas_call(
         functools.partial(layer_kernel, (peers, zs, rows, cols, ch)),
         out_shape=jax.ShapeDtypeStruct(frames.shape, BF16),
-        in_specs=[any_space, any_space, any_space, vmem, vmem, any_space],
-        out_specs=any_space,
+        in_specs=[in_hbm] * 6,
+        out_specs=vmem,
         scratch_shapes=[
-            pltpu.VMEM((count, rows, cols, ch), BF16),
             pltpu.VMEM((count * rows, 32, ch), F32),
             pltpu.VMEM((count, rows + 2, cols, 3 * ch), BF16),
             pltpu.VMEM((count, rows + 2, cols, 3 * ch), BF16),
@@ -265,28 +324,34 @@
             pltpu.VMEM((3, 3 * ch, ch), BF16),
             pieces, pieces, pieces, pieces,
             pltpu.VMEM((n, cols, lanes), F32),
-            pltpu.VMEM((count, rows, cols, ch), BF16),
+            pltpu.VMEM((1, ch), jnp.int32),
+            pltpu.VMEM((1, ch), F32),
             pltpu.VMEM((1, ch), F32),
             pltpu.VMEM((split, 1, lanes), F32),
             pltpu.VMEM((2, count, rows, ch), BF16),
             pltpu.VMEM((2, count, rows, ch), BF16),
             pltpu.VMEM((n, 2, count, step, ch), BF16),
             pltpu.VMEM((n, 2, count, step, ch), BF16),
-            dma, dma((3,)), dma((3,)), dma((n,)), dma((n,)),
+            dma, dma((2,)), dma((3,)), dma((3,)), dma((n,)), pltpu.SemaphoreType.REGULAR((3,)),
             dma((n + 1, 2)), dma((n + 1, 2)), dma((2,)), dma((2,)),
             dma((n,)), dma((n,)), dma((n,)), dma((n,)),
         ],
         compiler_params=pltpu.CompilerParams(
-            collective_id=0, has_side_effects=True, vmem_limit_bytes=56 << 20
+            collective_id=0, has_side_effects=True, vmem_limit_bytes=40 << 20
         ),
         name="layer",
     )(
-        frames,
-        input_weight.reshape(3, 3 * ch, ch),
-        output_weight.reshape(3, 3 * ch, ch),
-        pole_index.reshape(1, ch),
-        gelu_scale.reshape(1, ch),
-        start_state,
+        *(
+            pltpu.with_memory_space_constraint(array, pltpu.HBM)
+            for array in (
+                frames,
+                input_weight.reshape(3, 3 * ch, ch),
+                output_weight.reshape(3, 3 * ch, ch),
+                pole_index.reshape(1, ch),
+                gelu_scale.reshape(1, ch),
+                start_state,
+            )
+        )
     )
 
 

time: 46.7 us -> 40.2 us (0.86)
  the two profiles are of different devices: /device:TPU:1 before, /device:TPU:32 now
where the time goes in v2:
time: 40.2 us; the launch traced here: 39.5 us
  Pallas kernels  38.5 us (96%)
  local copies, waits for them, and re-layouts  0.97 us (2%)
    pallas_call x1, Pallas kernels, on_device(): pl.pallas_call(functools.partial(layer_kernel, (peers, zs, rows, cols, ch...  38.5 us
    unnamed x1, local copies, waits for them, and re-layouts  0.97 us

profile of v2, /device:TPU:32, one launch (start us, length us, event | category | flops | bytes accessed | tf_op | source)
XLA Modules:
  0.0 39.5 jit_solution(10964141134342378599)
XLA Ops:
  0.0 38.5 %layer.1 = bf16[2,32,16,512]{3,2,1,0:T(8,128)(2,1)S(1)} custom-call(bf16[2,32,16,512]{3,2,1,0:T(8,128)(2,1)} %frames_hbm.1, bf16[3,1536,512]{2,1,0:T(8,128)(2,1)} %bitcast.4, bf16[3,1536,512]{2,1,0:T(8,128)(2,1)} %bitcast.5, s32[1,512]{1,0:T(1,128)} %bitcast.6, f32[1,512]{1,0:T(1,128)} %bitcast.7, f32[32,16,512]{2,1,0:T(8,128)} %start_hbm.1), custom_call_target="tpu_custom_call" | custom-call | tf_op jit(solution)/shard_map/layer/pallas_call | solution.py:313
  38.5 1.0 %copy.8 = bf16[2,32,16,512]{3,2,1,0:T(8,128)(2,1)} copy(bf16[2,32,16,512]{3,2,1,0:T(8,128)(2,1)S(1)} %layer.1) | data formatting | bytes 2097152

commit v3 on v2

--- a/solution.py
+++ b/solution.py
@@ -19,9 +19,9 @@
     sizes,
     frames_hbm, w1_hbm, w2_hbm, pole_hbm, scale_hbm, start_hbm, out,
     wide, xf, xm, drive, w1, w2, ends, gathered, prefixes, carried, first, pole_ref, scale_ref,
-    decay_ref, decay2_ref, edge_out, edge_in, side_out, side_in,
+    decay_ref, decay2_ref, edge_out, edge_in, side_out, side_in, corner_out, corner_in, centers,
     frame_sem, small_sem, w1_sem, w2_sem, first_sem, near_sem,
-    col_send, col_recv, row_send, row_recv,
+    col_send, col_recv, row_send, row_recv, corner_send, corner_recv,
     end_send, end_recv, pre_send, pre_recv,
 ):
     peers, zs, rows, cols, ch = sizes
@@ -36,14 +36,15 @@
     piece_row, piece_part = me // split, lax.rem(me, split)
 
     def row_of(lo, hi):
-        return jnp.where(sx == 0, rows - hi, lo)
+        return jnp.where(sx == 0, lo, rows - hi)
 
     def base(c):
         return row_of(c * step, (c + 1) * step)
 
     border = jnp.where(sx == 0, rows, 1)
     blank = jnp.where(sx == 0, 0, rows + 1)
-    halo_there = jnp.where(sx == 0, 0, rows + 1)
+    halo_there = blank
+    halo_here = rows + 1 - blank
 
     mid = pl.ds(ch, ch)
     frame_copy = pltpu.make_async_copy(frames_hbm, xf.at[:, pl.ds(1, rows), :, mid], frame_sem)
@@ -72,8 +73,9 @@
         {"tm": lax.rem(y + 1, side) * side + x},
         {"tm": lax.rem(y + side - 1, side) * side + x},
     ]
+    diagonal = [{"sx": other, "sy": right}, {"sx": other, "sy": left}]
     barrier = pltpu.get_barrier_semaphore()
-    for where in [{"sy": left}, {"sy": right}, {"sx": other}] + around:
+    for where in diagonal + [{"sy": left}, {"sy": right}, {"sx": other}] + around:
         pl.semaphore_signal(barrier, inc=1, device_id=where, device_id_type=MESH)
 
     def tell(k):
@@ -99,7 +101,7 @@
         padded[:, pl.ds(blank, 1)] = jnp.zeros((2, 1, cols, 3 * ch), BF16)
 
     def side_refs(slot):
-        return (edge_out, edge_in) if slot == n else (side_out.at[slot], side_in.at[slot])
+        return (edge_out.at[slot - n], edge_in.at[slot - n]) if slot >= n else (side_out.at[slot], side_in.at[slot])
 
     def side_copies(slot):
         src, dst = side_refs(slot)
@@ -113,10 +115,40 @@
 
     def row_copy(padded, slot):
         return pltpu.make_async_remote_copy(
-            padded.at[:, pl.ds(border, 1)], padded.at[:, pl.ds(halo_there, 1)],
+            padded.at[:, pl.ds(border, 1), :, mid], padded.at[:, pl.ds(halo_there, 1), :, mid],
             row_send.at[slot], row_recv.at[slot],
             device_id={"sx": other}, device_id_type=MESH,
         )
+
+    def border_copies(padded, slot):
+        return [row_copy(padded, slot)] + [
+            pltpu.make_async_remote_copy(
+                corner_out.at[slot, d], corner_in.at[slot, d], corner_send.at[slot, d], corner_recv.at[slot, d],
+                device_id=to, device_id_type=MESH,
+            )
+            for d, to in enumerate(diagonal)
+        ]
+
+    def fill_corners(slot):
+        for d, col in ((0, 7 + cols), (1, 8)):
+            corner_out[slot, d] = jnp.concatenate(
+                [wide[f * rows + border - 1, col : col + 1, :] for f in range(2)], axis=0
+            ).astype(BF16)
+
+    def place_border(padded, slot, copies):
+        for copy in copies:
+            sent.append(copy.wait_send)
+        for copy in copies[slot:]:
+            copy.wait_recv()
+        for f in range(2):
+            at = 2 * rows + f
+            wide[at, 8 : 8 + cols, :] = padded[f, halo_here, :, ch : 2 * ch].astype(F32)
+            for d, col, kept in ((0, 7, z > 0), (1, 8 + cols, z < zs - 1)):
+                wide[at, col : col + 1, :] = jnp.where(kept, corner_in[slot, d].astype(F32)[f : f + 1], 0.0)
+            for j in (0, 2):
+                padded[f, halo_here, :, j * ch : (j + 1) * ch] = wide[at, 7 + j : 7 + j + cols, :].astype(BF16)
+
+    sent = []
 
     def send_sides(slot, at, count):
         src = side_refs(slot)[0]
@@ -126,7 +158,8 @@
             src[0, f] = last.astype(BF16)
             src[1, f] = head.astype(BF16)
         if slot == n:
-            pl.semaphore_wait(barrier, 3 + len(around))
+            fill_corners(0)
+            pl.semaphore_wait(barrier, 5 + len(around))
             tell(0)
         copies = side_copies(slot)
         for copy in copies:
@@ -165,7 +198,12 @@
         return 0
 
     lax.fori_loop(0, rows, widen, 0, unroll=4)
-    edges = send_sides(n, 0, rows)
+    half = rows // 2
+    early = send_sides(n, row_of(0, half), half)
+    late = send_sides(n + 1, row_of(half, rows), half)
+    border_f = border_copies(xf, 0)
+    for copy in border_f:
+        copy.start()
     for copy in small_copies:
         copy.wait()
     decay = jnp.exp(-0.001 * jnp.exp(pole_ref[...].astype(F32) * (math.log(300.0) / (NPOLES - 1))))
@@ -173,26 +211,16 @@
     for part in range(split):
         decay2_ref[part] = (decay * decay)[:, part * lanes : (part + 1) * lanes]
     w1_copies[1].wait()
-    drive[1] = dots(xf, w1, base(1), step, (1,))
-    hear(0)
-    tell(1)
-    for c in range(2, n - 1):
+    for c in range(n - 1):
         drive[c] = dots(xf, w1, base(c), step, (1,))
-    hear(1)
-    tell(2)
-    for copy in edges:
+        if c < 2:
+            hear(c)
+            tell(c + 1)
+    for copy in early:
         copy.wait_recv()
-    place_sides(n, 0, rows)
-    spread(xf, base(0), step)
-    row_f = row_copy(xf, 0)
-    row_f.start()
-    sent = [copy.wait_send for copy in edges] + [row_f.wait_send]
-
-    def rest(c, _):
-        spread(xf, base(c), step)
-        return 0
-
-    lax.fori_loop(1, n, rest, 0)
+        sent.append(copy.wait_send)
+    place_sides(n, row_of(0, half), half)
+    spread(xf, row_of(0, step + 1), step + 1)
     w1_copies[0].wait()
     w1_copies[2].wait()
 
@@ -210,9 +238,7 @@
         sent.append(all_of(src.at[c, pl.ds(0, peers - 1)], send.at[c]).wait)
 
     def drive_chunk(c):
-        if c == 0:
-            row_f.wait_recv()
-        if 1 <= c < n - 1:
+        if c < n - 1:
             got = drive[c] + dots(xf, w1, base(c), step, (0, 2))
         else:
             got = dots(xf, w1, base(c), step, (0, 1, 2))
@@ -221,7 +247,7 @@
         for r in range(step):
             for part in range(split):
                 ends[c, r * split + part] = end[r, :, part * lanes : (part + 1) * lanes].astype(BF16)
-        if c == 1:
+        if c == 0:
             hear(2)
         exchange(ends, gathered, end_send, end_recv, c)
 
@@ -246,10 +272,14 @@
                 mixed = jax.nn.gelu(scale_ref[...] * state)
                 wide[f * rows + at + r, 8 : 8 + cols, :] = mixed
                 xm[f, at + r + 1, :, ch : 2 * ch] = mixed.astype(BF16)
+        if c == n - 1:
+            fill_corners(1)
+            for copy in border_m:
+                copy.start()
         sides[c] = send_sides(c, at, step)
 
     sides = {}
-    row_m = row_copy(xm, 1)
+    border_m = border_copies(xm, 1)
 
     def lay_chunk(c):
         at = base(c)
@@ -258,43 +288,54 @@
             sent.append(copy.wait_send)
         place_sides(c, at, step)
         spread(xm, at, step)
-        if c == 0:
-            row_m.start()
-            sent.append(row_m.wait_send)
-
-    def result_chunk(c):
+
+    def window(c):
         lo = max(c * step - 1, 0)
         hi = rows if c == n - 1 else (c + 1) * step - 1
-        at = row_of(lo, hi)
+        return row_of(lo, hi), hi - lo
+
+    def center_chunk(c):
+        at, count = window(c)
         if c == n - 1:
-            part = dots(xm, w2, at, hi - lo, (1,))
-            lay_chunk(c)
-            got = part + dots(xm, w2, at, hi - lo, (0, 2))
-        else:
-            got = dots(xm, w2, at, hi - lo, (0, 1, 2))
-        out[:, pl.ds(at, hi - lo)] = got.astype(BF16)
-
+            border_m[0].wait_recv()
+        centers[c, :, pl.ds(0, count)] = dots(xm, w2, at, count, (1,))
+
+    def result_chunk(c):
+        at, count = window(c)
+        got = centers[c, :, pl.ds(0, count)] + dots(xm, w2, at, count, (0, 2))
+        out[:, pl.ds(at, count)] = got.astype(BF16)
+
+    drive_chunk(0)
+    for copy in late:
+        copy.wait_recv()
+        sent.append(copy.wait_send)
+    place_sides(n + 1, row_of(half, rows), half)
+    spread(xf, row_of(step + 1, 2 * step + 1), step)
     drive_chunk(1)
-    drive_chunk(0)
+    spread(xf, row_of(2 * step + 1, rows), rows - 2 * step - 1)
     drive_chunk(2)
-    prefix_chunk(1)
+    place_border(xf, 0, border_f)
     drive_chunk(3)
-    prefix_chunk(0)
-    prefix_chunk(2)
-    mix_chunk(1)
-    prefix_chunk(3)
-    mix_chunk(0)
+    for c in range(n):
+        prefix_chunk(c)
     for copy in w2_copies:
         copy.wait()
+    mix_chunk(0)
+    center_chunk(0)
+    mix_chunk(1)
+    center_chunk(1)
+    mix_chunk(2)
+    center_chunk(2)
+    lay_chunk(0)
+    result_chunk(0)
+    mix_chunk(3)
     lay_chunk(1)
-    lay_chunk(0)
-    mix_chunk(2)
     result_chunk(1)
-    row_m.wait_recv()
-    result_chunk(0)
     lay_chunk(2)
-    mix_chunk(3)
     result_chunk(2)
+    center_chunk(3)
+    place_border(xm, 1, border_m)
+    lay_chunk(3)
     result_chunk(3)
     for wait in sent:
         wait()
@@ -316,7 +357,7 @@
         in_specs=[in_hbm] * 6,
         out_specs=vmem,
         scratch_shapes=[
-            pltpu.VMEM((count * rows, 32, ch), F32),
+            pltpu.VMEM((count * rows + count, 32, ch), F32),
             pltpu.VMEM((count, rows + 2, cols, 3 * ch), BF16),
             pltpu.VMEM((count, rows + 2, cols, 3 * ch), BF16),
             pltpu.VMEM((n, count, step, cols, ch), F32),
@@ -328,16 +369,19 @@
             pltpu.VMEM((1, ch), F32),
             pltpu.VMEM((1, ch), F32),
             pltpu.VMEM((split, 1, lanes), F32),
-            pltpu.VMEM((2, count, rows, ch), BF16),
-            pltpu.VMEM((2, count, rows, ch), BF16),
+            pltpu.VMEM((2, 2, count, rows // 2, ch), BF16),
+            pltpu.VMEM((2, 2, count, rows // 2, ch), BF16),
             pltpu.VMEM((n, 2, count, step, ch), BF16),
             pltpu.VMEM((n, 2, count, step, ch), BF16),
+            pltpu.VMEM((2, 2, count, ch), BF16),
+            pltpu.VMEM((2, 2, count, ch), BF16),
+            pltpu.VMEM((n, count, step + 1, cols, ch), F32),
             dma, dma((2,)), dma((3,)), dma((3,)), dma((n,)), pltpu.SemaphoreType.REGULAR((3,)),
-            dma((n + 1, 2)), dma((n + 1, 2)), dma((2,)), dma((2,)),
+            dma((n + 2, 2)), dma((n + 2, 2)), dma((2,)), dma((2,)), dma((2, 2)), dma((2, 2)),
             dma((n,)), dma((n,)), dma((n,)), dma((n,)),
         ],
         compiler_params=pltpu.CompilerParams(
-            collective_id=0, has_side_effects=True, vmem_limit_bytes=40 << 20
+            collective_id=0, has_side_effects=True, vmem_limit_bytes=44 << 20
         ),
         name="layer",
     )(

time: 40.2 us -> 36.1 us (0.90)
  the two profiles are of different devices: /device:TPU:32 before, /device:TPU:1 now
where the time goes in v3:
time: 36.1 us; the launch traced here: 36 us
  Pallas kernels  35 us (97%)
  local copies, waits for them, and re-layouts  0.97 us (3%)
    pallas_call x1, Pallas kernels, on_device(): pl.pallas_call(functools.partial(layer_kernel, (peers, zs, rows, cols, ch...  35 us
    unnamed x1, local copies, waits for them, and re-layouts  0.97 us

profile of v3, /device:TPU:1, one launch (start us, length us, event | category | flops | bytes accessed | tf_op | source)
XLA Modules:
  0.0 36.0 jit_solution(9424381596589302231)
XLA Ops:
  0.0 35.0 %layer.1 = bf16[2,32,16,512]{3,2,1,0:T(8,128)(2,1)S(1)} custom-call(bf16[2,32,16,512]{3,2,1,0:T(8,128)(2,1)} %frames_hbm.1, bf16[3,1536,512]{2,1,0:T(8,128)(2,1)} %bitcast.4, bf16[3,1536,512]{2,1,0:T(8,128)(2,1)} %bitcast.5, s32[1,512]{1,0:T(1,128)} %bitcast.6, f32[1,512]{1,0:T(1,128)} %bitcast.7, f32[32,16,512]{2,1,0:T(8,128)} %start_hbm.1), custom_call_target="tpu_custom_call" | custom-call | tf_op jit(solution)/shard_map/layer/pallas_call | solution.py:354
  35.0 1.0 %copy.8 = bf16[2,32,16,512]{3,2,1,0:T(8,128)(2,1)} copy(bf16[2,32,16,512]{3,2,1,0:T(8,128)(2,1)S(1)} %layer.1) | data formatting | bytes 2097152

commit v4 on v3

--- a/solution.py
+++ b/solution.py
@@ -33,6 +33,14 @@
     me, sx, z = lax.axis_index("tm"), lax.axis_index("sx"), lax.axis_index("sy")
     other = 1 - sx
     right, left = lax.rem(z + 1, zs), lax.rem(z + zs - 1, zs)
+    has_left, has_right = z > 0, z < zs - 1
+    goes, comes = (has_right, has_left), (has_left, has_right)
+
+    def only(condition, action):
+        def run():
+            pl.when(condition)(lambda: action() and None)
+        return run
+
     piece_row, piece_part = me // split, lax.rem(me, split)
 
     def row_of(lo, hi):
@@ -46,15 +54,47 @@
     halo_there = blank
     halo_here = rows + 1 - blank
 
+    y, x = me // side, lax.rem(me, side)
+    in_row = [{"tm": y * side + lax.rem(x + k, side)} for k in range(1, side)]
+    in_column = [{"tm": lax.rem(y + k, side) * side + x} for k in range(1, side)]
+    around = in_row + in_column
+    diagonal = [{"sx": other, "sy": right}, {"sx": other, "sy": left}]
+    barrier = pltpu.get_barrier_semaphore()
+    for where in [{"sx": other}] + around:
+        pl.semaphore_signal(barrier, inc=1, device_id=where, device_id_type=MESH)
+    for condition, to, corner in ((has_right, right, diagonal[0]), (has_left, left, diagonal[1])):
+        @pl.when(condition)
+        def _(to=to, corner=corner):
+            for where in ({"sy": to}, corner):
+                pl.semaphore_signal(barrier, inc=1, device_id=where, device_id_type=MESH)
+    expected = 1 + len(around) + 2 * jnp.where(has_left, 1, 0) + 2 * jnp.where(has_right, 1, 0)
+
     mid = pl.ds(ch, ch)
-    frame_copy = pltpu.make_async_copy(frames_hbm, xf.at[:, pl.ds(1, rows), :, mid], frame_sem)
-    frame_copy.start()
+    quarter = rows // 4
+    for f in range(2):
+        for part in range(4):
+            pltpu.make_async_copy(
+                frames_hbm.at[f, pl.ds(part * quarter, quarter)],
+                xf.at[f, pl.ds(1 + part * quarter, quarter), :, mid], frame_sem,
+            ).start()
+
+    class Weight:
+        def __init__(self, src, dst, sem, j):
+            self.copies = [
+                pltpu.make_async_copy(src.at[i, pl.ds(j * ch, ch)], dst.at[i, pl.ds(j * ch, ch)], sem)
+                for i in range(3)
+            ]
+            self.whole = pltpu.make_async_copy(src.at[:, pl.ds(j * ch, ch)], dst.at[:, pl.ds(j * ch, ch)], sem)
+
+        def start(self):
+            for copy in self.copies:
+                copy.start()
+
+        def wait(self):
+            self.whole.wait()
 
     def weight_copies(src, dst, sems):
-        return [
-            pltpu.make_async_copy(src.at[:, pl.ds(j * ch, ch)], dst.at[:, pl.ds(j * ch, ch)], sems.at[j])
-            for j in range(3)
-        ]
+        return [Weight(src, dst, sems.at[j], j) for j in range(3)]
 
     small_copies = [
         pltpu.make_async_copy(pole_hbm, pole_ref, small_sem.at[0]),
@@ -63,27 +103,14 @@
     for copy in small_copies:
         copy.start()
     w1_copies = weight_copies(w1_hbm, w1, w1_sem)
-    for j in (1, 0, 2):
-        w1_copies[j].start()
-
-    y, x = me // side, lax.rem(me, side)
-    around = [
-        {"tm": y * side + lax.rem(x + 1, side)},
-        {"tm": y * side + lax.rem(x + side - 1, side)},
-        {"tm": lax.rem(y + 1, side) * side + x},
-        {"tm": lax.rem(y + side - 1, side) * side + x},
-    ]
-    diagonal = [{"sx": other, "sy": right}, {"sx": other, "sy": left}]
-    barrier = pltpu.get_barrier_semaphore()
-    for where in diagonal + [{"sy": left}, {"sy": right}, {"sx": other}] + around:
-        pl.semaphore_signal(barrier, inc=1, device_id=where, device_id_type=MESH)
-
-    def tell(k):
-        for where in around:
-            pl.semaphore_signal(near_sem.at[k], inc=1, device_id=where, device_id_type=MESH)
-
-    def hear(k):
-        pl.semaphore_wait(near_sem.at[k], len(around))
+    w1_copies[1].start()
+
+    def tell():
+        for where in in_row:
+            pl.semaphore_signal(near_sem, inc=1, device_id=where, device_id_type=MESH)
+
+    def hear():
+        pl.semaphore_wait(near_sem, len(in_row))
 
     first_copies = []
     for c in range(n):
@@ -94,9 +121,13 @@
         copy.start()
         first_copies.append(copy)
     w2_copies = weight_copies(w2_hbm, w2, w2_sem)
-    for copy in w2_copies:
-        copy.start()
-
+
+    for d in range(2):
+        @pl.when(jnp.logical_not(comes[d]))
+        def _(d=d):
+            edge_in[:, d] = jnp.zeros_like(edge_in[:, d])
+            side_in[:, d] = jnp.zeros_like(side_in[:, d])
+            corner_in[:, d] = jnp.zeros_like(corner_in[:, d])
     for padded in (xf, xm):
         padded[:, pl.ds(blank, 1)] = jnp.zeros((2, 1, cols, 3 * ch), BF16)
 
@@ -129,6 +160,11 @@
             for d, to in enumerate(diagonal)
         ]
 
+    def start_border(copies):
+        copies[0].start()
+        for d, copy in enumerate(copies[1:]):
+            only(goes[d], copy.start)()
+
     def fill_corners(slot):
         for d, col in ((0, 7 + cols), (1, 8)):
             corner_out[slot, d] = jnp.concatenate(
@@ -136,19 +172,23 @@
             ).astype(BF16)
 
     def place_border(padded, slot, copies):
-        for copy in copies:
-            sent.append(copy.wait_send)
-        for copy in copies[slot:]:
-            copy.wait_recv()
+        sent.append(copies[0].wait_send)
+        if slot == 0:
+            copies[0].wait_recv()
+        take(copies[1:])
         for f in range(2):
             at = 2 * rows + f
             wide[at, 8 : 8 + cols, :] = padded[f, halo_here, :, ch : 2 * ch].astype(F32)
-            for d, col, kept in ((0, 7, z > 0), (1, 8 + cols, z < zs - 1)):
-                wide[at, col : col + 1, :] = jnp.where(kept, corner_in[slot, d].astype(F32)[f : f + 1], 0.0)
+            for d, col in ((0, 7), (1, 8 + cols)):
+                wide[at, col : col + 1, :] = corner_in[slot, d].astype(F32)[f : f + 1]
             for j in (0, 2):
                 padded[f, halo_here, :, j * ch : (j + 1) * ch] = wide[at, 7 + j : 7 + j + cols, :].astype(BF16)
 
     sent = []
+
+    def flush(kept=0):
+        while len(sent) > kept:
+            sent.pop(0)()
 
     def send_sides(slot, at, count):
         src = side_refs(slot)[0]
@@ -159,19 +199,24 @@
             src[1, f] = head.astype(BF16)
         if slot == n:
             fill_corners(0)
-            pl.semaphore_wait(barrier, 5 + len(around))
-            tell(0)
+            pl.semaphore_wait(barrier, expected)
+            tell()
         copies = side_copies(slot)
-        for copy in copies:
-            copy.start()
+        for d, copy in enumerate(copies):
+            only(goes[d], copy.start)()
         return copies
+
+    def take(copies):
+        for d, copy in enumerate(copies):
+            only(comes[d], copy.wait_recv)()
+            sent.append(only(goes[d], copy.wait_send))
 
     def place_sides(slot, at, count):
         dst = side_refs(slot)[1]
         for f in range(2):
             spot = pl.ds(f * rows + at, count)
-            for d, col, kept in ((0, 7, z > 0), (1, 8 + cols, z < zs - 1)):
-                wide[spot, col, :] = jnp.where(kept, dst[d, f].astype(F32), 0.0)
+            for d, col in ((0, 7), (1, 8 + cols)):
+                wide[spot, col, :] = dst[d, f].astype(F32)
 
     def spread(padded, at, count):
         for f in range(2):
@@ -190,7 +235,9 @@
         right_side = jnp.concatenate([weight[i, j * ch : (j + 1) * ch] for i in range(3) for j in js], axis=0)
         return jnp.dot(left_side, right_side, preferred_element_type=F32).reshape(2, count, cols, ch)
 
-    frame_copy.wait()
+    pltpu.make_async_copy(frames_hbm, xf.at[:, pl.ds(1, rows), :, mid], frame_sem).wait()
+    w1_copies[0].start()
+    w1_copies[2].start()
 
     def widen(r, _):
         for f in range(2):
@@ -202,8 +249,7 @@
     early = send_sides(n, row_of(0, half), half)
     late = send_sides(n + 1, row_of(half, rows), half)
     border_f = border_copies(xf, 0)
-    for copy in border_f:
-        copy.start()
+    start_border(border_f)
     for copy in small_copies:
         copy.wait()
     decay = jnp.exp(-0.001 * jnp.exp(pole_ref[...].astype(F32) * (math.log(300.0) / (NPOLES - 1))))
@@ -213,12 +259,9 @@
     w1_copies[1].wait()
     for c in range(n - 1):
         drive[c] = dots(xf, w1, base(c), step, (1,))
-        if c < 2:
-            hear(c)
-            tell(c + 1)
-    for copy in early:
-        copy.wait_recv()
-        sent.append(copy.wait_send)
+    take(early)
+    for copy in w2_copies:
+        copy.start()
     place_sides(n, row_of(0, half), half)
     spread(xf, row_of(0, step + 1), step + 1)
     w1_copies[0].wait()
@@ -248,7 +291,7 @@
             for part in range(split):
                 ends[c, r * split + part] = end[r, :, part * lanes : (part + 1) * lanes].astype(BF16)
         if c == 0:
-            hear(2)
+            hear()
         exchange(ends, gathered, end_send, end_recv, c)
 
     def prefix_chunk(c):
@@ -263,6 +306,8 @@
         exchange(prefixes, carried, pre_send, pre_recv, c)
 
     def mix_chunk(c):
+        if c == 0:
+            flush(n)
         all_of(carried.at[c], pre_recv.at[c]).wait()
         at = base(c)
         for r in range(step):
@@ -274,8 +319,7 @@
                 xm[f, at + r + 1, :, ch : 2 * ch] = mixed.astype(BF16)
         if c == n - 1:
             fill_corners(1)
-            for copy in border_m:
-                copy.start()
+            start_border(border_m)
         sides[c] = send_sides(c, at, step)
 
     sides = {}
@@ -283,9 +327,7 @@
 
     def lay_chunk(c):
         at = base(c)
-        for copy in sides[c]:
-            copy.wait_recv()
-            sent.append(copy.wait_send)
+        take(sides[c])
         place_sides(c, at, step)
         spread(xm, at, step)
 
@@ -306,9 +348,7 @@
         out[:, pl.ds(at, count)] = got.astype(BF16)
 
     drive_chunk(0)
-    for copy in late:
-        copy.wait_recv()
-        sent.append(copy.wait_send)
+    take(late)
     place_sides(n + 1, row_of(half, rows), half)
     spread(xf, row_of(step + 1, 2 * step + 1), step)
     drive_chunk(1)
@@ -316,8 +356,10 @@
     drive_chunk(2)
     place_border(xf, 0, border_f)
     drive_chunk(3)
-    for c in range(n):
-        prefix_chunk(c)
+    prefix_chunk(0)
+    prefix_chunk(1)
+    prefix_chunk(2)
+    prefix_chunk(3)
     for copy in w2_copies:
         copy.wait()
     mix_chunk(0)
@@ -326,9 +368,9 @@
     center_chunk(1)
     mix_chunk(2)
     center_chunk(2)
+    mix_chunk(3)
     lay_chunk(0)
     result_chunk(0)
-    mix_chunk(3)
     lay_chunk(1)
     result_chunk(1)
     lay_chunk(2)
@@ -337,8 +379,7 @@
     place_border(xm, 1, border_m)
     lay_chunk(3)
     result_chunk(3)
-    for wait in sent:
-        wait()
+    flush()
 
 
 def on_device(peers, zs, frames, input_weight, output_weight, pole_index, gelu_scale, start_state):
@@ -376,7 +417,7 @@
             pltpu.VMEM((2, 2, count, ch), BF16),
             pltpu.VMEM((2, 2, count, ch), BF16),
             pltpu.VMEM((n, count, step + 1, cols, ch), F32),
-            dma, dma((2,)), dma((3,)), dma((3,)), dma((n,)), pltpu.SemaphoreType.REGULAR((3,)),
+            dma, dma((2,)), dma((3,)), dma((3,)), dma((n,)), pltpu.SemaphoreType.REGULAR,
             dma((n + 2, 2)), dma((n + 2, 2)), dma((2,)), dma((2,)), dma((2, 2)), dma((2, 2)),
             dma((n,)), dma((n,)), dma((n,)), dma((n,)),
         ],

time: 36.1 us -> 32.9 us (0.911)
  the two profiles are of different devices: /device:TPU:1 before, /device:TPU:32 now
where the time goes in v4:
time: 32.9 us; the launch traced here: 32.8 us
  Pallas kernels  31.8 us (97%)
  local copies, waits for them, and re-layouts  0.97 us (3%)
    pallas_call x1, Pallas kernels, on_device(): pl.pallas_call(functools.partial(layer_kernel, (peers, zs, rows, cols, ch...  31.8 us
    unnamed x1, local copies, waits for them, and re-layouts  0.97 us

profile of v4, /device:TPU:32, one launch (start us, length us, event | category | flops | bytes accessed | tf_op | source)
XLA Modules:
  0.0 32.8 jit_solution(17569126087503987186)
XLA Ops:
  0.0 31.8 %layer.1 = bf16[2,32,16,512]{3,2,1,0:T(8,128)(2,1)S(1)} custom-call(bf16[2,32,16,512]{3,2,1,0:T(8,128)(2,1)} %frames_hbm.1, bf16[3,1536,512]{2,1,0:T(8,128)(2,1)} %bitcast.4, bf16[3,1536,512]{2,1,0:T(8,128)(2,1)} %bitcast.5, s32[1,512]{1,0:T(1,128)} %bitcast.6, f32[1,512]{1,0:T(1,128)} %bitcast.7, f32[32,16,512]{2,1,0:T(8,128)} %start_hbm.1), custom_call_target="tpu_custom_call" | custom-call | tf_op jit(solution)/shard_map/layer/pallas_call | solution.py:395
  31.8 1.0 %copy.8 = bf16[2,32,16,512]{3,2,1,0:T(8,128)(2,1)} copy(bf16[2,32,16,512]{3,2,1,0:T(8,128)(2,1)S(1)} %layer.1) | data formatting | bytes 2097152

commit v5 on v4

--- a/solution.py
+++ b/solution.py
@@ -19,7 +19,7 @@
     sizes,
     frames_hbm, w1_hbm, w2_hbm, pole_hbm, scale_hbm, start_hbm, out,
     wide, xf, xm, drive, w1, w2, ends, gathered, prefixes, carried, first, pole_ref, scale_ref,
-    decay_ref, decay2_ref, edge_out, edge_in, side_out, side_in, corner_out, corner_in, centers,
+    decay_ref, decay2_ref, edge_out, edge_in, side_out, side_in, corner_out, corner_in, acc, beyond,
     frame_sem, small_sem, w1_sem, w2_sem, first_sem, near_sem,
     col_send, col_recv, row_send, row_recv, corner_send, corner_recv,
     end_send, end_recv, pre_send, pre_recv,
@@ -321,31 +321,71 @@
             fill_corners(1)
             start_border(border_m)
         sides[c] = send_sides(c, at, step)
+        spread(xm, at, step)
 
     sides = {}
     border_m = border_copies(xm, 1)
-
-    def lay_chunk(c):
-        at = base(c)
-        take(sides[c])
-        place_sides(c, at, step)
-        spread(xm, at, step)
 
     def window(c):
         lo = max(c * step - 1, 0)
         hi = rows if c == n - 1 else (c + 1) * step - 1
         return row_of(lo, hi), hi - lo
 
-    def center_chunk(c):
+    def gather_chunk(c, js, more=False):
         at, count = window(c)
-        if c == n - 1:
-            border_m[0].wait_recv()
-        centers[c, :, pl.ds(0, count)] = dots(xm, w2, at, count, (1,))
-
-    def result_chunk(c):
-        at, count = window(c)
-        got = centers[c, :, pl.ds(0, count)] + dots(xm, w2, at, count, (0, 2))
-        out[:, pl.ds(at, count)] = got.astype(BF16)
+        got = dots(xm, w2, at, count, js)
+        for f in range(2):
+            spot = pl.ds(f * rows + at, count)
+            acc[spot] = acc[spot] + got[f] if more else got[f]
+
+    def border_row():
+        border_m[0].wait_recv()
+        sent.append(border_m[0].wait_send)
+        for f in range(2):
+            at = 2 * rows + f
+            wide[at, 8 : 8 + cols, :] = xm[f, halo_here, :, ch : 2 * ch].astype(F32)
+            for j in (0, 2):
+                xm[f, halo_here, :, j * ch : (j + 1) * ch] = wide[at, 7 + j : 7 + j + cols, :].astype(BF16)
+
+    def clear_sides():
+        none = jnp.zeros((2 * rows + 2, ch), F32)
+        for col in (7, 8 + cols):
+            wide[:, col, :] = none
+
+    def beyond_chunk(c):
+        take(sides[c])
+        at = pl.multiple_of(base(c) + 8, 8)
+        for d in range(2):
+            for f in range(2):
+                beyond[d, f, pl.ds(at, step), :] = side_in[c, d, f].astype(F32)
+
+    def beyond_corners():
+        take(border_m[1:])
+        for d in range(2):
+            corner = corner_in[1, d].astype(F32)
+            for f in range(2):
+                row = corner[f : f + 1]
+                beyond[d, f, 7:8, :] = jnp.where(sx == 1, row, 0.0)
+                beyond[d, f, 8 + rows : 9 + rows, :] = jnp.where(sx == 0, row, 0.0)
+
+    def finish():
+        for d, j, col in ((0, 0, 0), (1, 2, cols - 1)):
+            left_side = jnp.concatenate(
+                [
+                    jnp.concatenate([beyond[d, f, 7 + i : 7 + i + rows, :].astype(BF16) for i in range(3)], axis=-1)
+                    for f in range(2)
+                ],
+                axis=0,
+            )
+            right_side = jnp.concatenate([w2[i, j * ch : (j + 1) * ch] for i in range(3)], axis=0)
+            acc[:, col, :] = acc[:, col, :] + jnp.dot(left_side, right_side, preferred_element_type=F32)
+
+        def narrow(r, _):
+            for f in range(2):
+                out[f, r] = acc[f * rows + r].astype(BF16)
+            return 0
+
+        lax.fori_loop(0, rows, narrow, 0, unroll=8)
 
     drive_chunk(0)
     take(late)
@@ -356,29 +396,28 @@
     drive_chunk(2)
     place_border(xf, 0, border_f)
     drive_chunk(3)
-    prefix_chunk(0)
-    prefix_chunk(1)
-    prefix_chunk(2)
-    prefix_chunk(3)
+    clear_sides()
+    for c in range(n):
+        prefix_chunk(c)
     for copy in w2_copies:
         copy.wait()
+    every = (0, 1, 2)
     mix_chunk(0)
-    center_chunk(0)
+    gather_chunk(0, every)
     mix_chunk(1)
-    center_chunk(1)
+    gather_chunk(1, (1,))
     mix_chunk(2)
-    center_chunk(2)
+    gather_chunk(2, (1,))
     mix_chunk(3)
-    lay_chunk(0)
-    result_chunk(0)
-    lay_chunk(1)
-    result_chunk(1)
-    lay_chunk(2)
-    result_chunk(2)
-    center_chunk(3)
-    place_border(xm, 1, border_m)
-    lay_chunk(3)
-    result_chunk(3)
+    gather_chunk(1, (0, 2), True)
+    gather_chunk(2, (0, 2), True)
+    border_row()
+    gather_chunk(3, every)
+    flush()
+    for c in range(n):
+        beyond_chunk(c)
+    beyond_corners()
+    finish()
     flush()
 
 
@@ -416,7 +455,8 @@
             pltpu.VMEM((n, 2, count, step, ch), BF16),
             pltpu.VMEM((2, 2, count, ch), BF16),
             pltpu.VMEM((2, 2, count, ch), BF16),
-            pltpu.VMEM((n, count, step + 1, cols, ch), F32),
+            pltpu.VMEM((count * rows, cols, ch), F32),
+            pltpu.VMEM((2, count, rows + 16, ch), F32),
             dma, dma((2,)), dma((3,)), dma((3,)), dma((n,)), pltpu.SemaphoreType.REGULAR,
             dma((n + 2, 2)), dma((n + 2, 2)), dma((2,)), dma((2,)), dma((2, 2)), dma((2, 2)),
             dma((n,)), dma((n,)), dma((n,)), dma((n,)),

time: 32.9 us -> 31.9 us (0.970)
  Pallas kernels: 31.8 us -> 30.8 us
    pallas_call x1, Pallas kernels: 31.8 us -> 30.8 us  [on_device(): pl.pallas_call(functools.partial(layer_kernel, (peers, zs, rows, cols, ch...]
where the time goes in v5:
time: 31.9 us; the launch traced here: 31.8 us
  Pallas kernels  30.8 us (97%)
  local copies, waits for them, and re-layouts  0.97 us (3%)
    pallas_call x1, Pallas kernels, on_device(): pl.pallas_call(functools.partial(layer_kernel, (peers, zs, rows, cols, ch...  30.8 us
    unnamed x1, local copies, waits for them, and re-layouts  0.97 us

profile of v5, /device:TPU:32, one launch (start us, length us, event | category | flops | bytes accessed | tf_op | source)
XLA Modules:
  0.0 31.8 jit_solution(11735704655417913863)
XLA Ops:
  0.0 30.8 %layer.1 = bf16[2,32,16,512]{3,2,1,0:T(8,128)(2,1)S(1)} custom-call(bf16[2,32,16,512]{3,2,1,0:T(8,128)(2,1)} %frames_hbm.1, bf16[3,1536,512]{2,1,0:T(8,128)(2,1)} %bitcast.4, bf16[3,1536,512]{2,1,0:T(8,128)(2,1)} %bitcast.5, s32[1,512]{1,0:T(1,128)} %bitcast.6, f32[1,512]{1,0:T(1,128)} %bitcast.7, f32[32,16,512]{2,1,0:T(8,128)} %start_hbm.1), custom_call_target="tpu_custom_call" | custom-call | tf_op jit(solution)/shard_map/layer/pallas_call | solution.py:434
  30.8 1.0 %copy.8 = bf16[2,32,16,512]{3,2,1,0:T(8,128)(2,1)} copy(bf16[2,32,16,512]{3,2,1,0:T(8,128)(2,1)S(1)} %layer.1) | data formatting | bytes 2097152

commit v6 on v5

--- a/solution.py
+++ b/solution.py
@@ -19,8 +19,8 @@
     sizes,
     frames_hbm, w1_hbm, w2_hbm, pole_hbm, scale_hbm, start_hbm, out,
     wide, xf, xm, drive, w1, w2, ends, gathered, prefixes, carried, first, pole_ref, scale_ref,
-    decay_ref, decay2_ref, edge_out, edge_in, side_out, side_in, corner_out, corner_in, acc, beyond,
-    frame_sem, small_sem, w1_sem, w2_sem, first_sem, near_sem,
+    decay_ref, decay2_ref, edge_out, edge_in, side_out, side_in, corner_out, corner_in, acc, beyond, tile,
+    frame_sem, small_sem, w1_sem, w2_sem, first_sem, tile_sem, near_sem,
     col_send, col_recv, row_send, row_recv, corner_send, corner_recv,
     end_send, end_recv, pre_send, pre_recv,
 ):
@@ -262,6 +262,8 @@
     take(early)
     for copy in w2_copies:
         copy.start()
+    tile_copy = pltpu.make_async_copy(start_hbm, tile, tile_sem)
+    only(me == 0, tile_copy.start)()
     place_sides(n, row_of(0, half), half)
     spread(xf, row_of(0, step + 1), step + 1)
     w1_copies[0].wait()
@@ -270,15 +272,36 @@
     def all_of(ref, sem):
         return pltpu.make_async_copy(ref, ref, sem)
 
-    def exchange(src, dst, send, recv, c):
-        pltpu.make_async_copy(src.at[c, me], dst.at[c, me], recv.at[c]).start()
+    def transfer(src, dst, send, recv, c, to):
+        return pltpu.make_async_remote_copy(
+            src.at[c, to], dst.at[c, me], send.at[c], recv.at[c], device_id={"tm": to}, device_id_type=MESH
+        )
+
+    is_last, is_first = me == peers - 1, me == 0
+
+    def send_ends(c):
+        @pl.when(jnp.logical_not(is_last))
+        def _():
+            pltpu.make_async_copy(ends.at[c, me], gathered.at[c, me], end_recv.at[c]).start()
+            for k in range(1, peers):
+                transfer(ends, gathered, end_send, end_recv, c, lax.rem(me + k, peers)).start()
+
+        sent.append(only(jnp.logical_not(is_last), all_of(ends.at[c, pl.ds(0, peers - 1)], end_send.at[c]).wait))
+
+    def send_prefixes(c):
+        @pl.when(jnp.logical_not(is_first))
+        def _():
+            pltpu.make_async_copy(prefixes.at[c, me], carried.at[c, me], pre_recv.at[c]).start()
+
         for k in range(1, peers):
             to = lax.rem(me + k, peers)
-            pltpu.make_async_remote_copy(
-                src.at[c, to], dst.at[c, me], send.at[c], recv.at[c],
-                device_id={"tm": to}, device_id_type=MESH,
-            ).start()
-        sent.append(all_of(src.at[c, pl.ds(0, peers - 1)], send.at[c]).wait)
+            only(to != 0, transfer(prefixes, carried, pre_send, pre_recv, c, to).start)()
+
+        def settle():
+            only(is_first, all_of(prefixes.at[c, pl.ds(0, peers - 1)], pre_send.at[c]).wait)()
+            only(jnp.logical_not(is_first), all_of(prefixes.at[c, pl.ds(0, peers - 2)], pre_send.at[c]).wait)()
+
+        sent.append(settle)
 
     def drive_chunk(c):
         if c < n - 1:
@@ -292,23 +315,23 @@
                 ends[c, r * split + part] = end[r, :, part * lanes : (part + 1) * lanes].astype(BF16)
         if c == 0:
             hear()
-        exchange(ends, gathered, end_send, end_recv, c)
+        send_ends(c)
 
     def prefix_chunk(c):
         first_copies[c].wait()
-        all_of(gathered.at[c], end_recv.at[c]).wait()
+        all_of(gathered.at[c, pl.ds(0, peers - 1)], end_recv.at[c]).wait()
         square = decay2_ref[pl.ds(piece_part, 1)].reshape(1, lanes)
         state = first[c]
         for i in range(peers):
             prefixes[c, i] = state.astype(BF16)
             if i < peers - 1:
                 state = square * state + gathered[c, i].astype(F32)
-        exchange(prefixes, carried, pre_send, pre_recv, c)
+        send_prefixes(c)
 
     def mix_chunk(c):
         if c == 0:
             flush(n)
-        all_of(carried.at[c], pre_recv.at[c]).wait()
+        only(jnp.logical_not(is_first), all_of(carried.at[c], pre_recv.at[c]).wait)()
         at = base(c)
         for r in range(step):
             state = jnp.concatenate([carried[c, r * split + part] for part in range(split)], axis=-1).astype(F32)
@@ -397,6 +420,17 @@
     place_border(xf, 0, border_f)
     drive_chunk(3)
     clear_sides()
+
+    @pl.when(is_first)
+    def _():
+        tile_copy.wait()
+        for c in range(n):
+            for r in range(step):
+                for part in range(split):
+                    carried[c, r * split + part] = tile[
+                        base(c) + r, :, part * lanes : (part + 1) * lanes
+                    ].astype(BF16)
+
     for c in range(n):
         prefix_chunk(c)
     for copy in w2_copies:
@@ -457,7 +491,8 @@
             pltpu.VMEM((2, 2, count, ch), BF16),
             pltpu.VMEM((count * rows, cols, ch), F32),
             pltpu.VMEM((2, count, rows + 16, ch), F32),
-            dma, dma((2,)), dma((3,)), dma((3,)), dma((n,)), pltpu.SemaphoreType.REGULAR,
+            pltpu.VMEM((rows, cols, ch), F32),
+            dma, dma((2,)), dma((3,)), dma((3,)), dma((n,)), dma, pltpu.SemaphoreType.REGULAR,
             dma((n + 2, 2)), dma((n + 2, 2)), dma((2,)), dma((2,)), dma((2, 2)), dma((2, 2)),
             dma((n,)), dma((n,)), dma((n,)), dma((n,)),
         ],

time: 31.9 us -> 30.9 us (0.969); the launches traced: 31.8 us -> 30.3 us
  Pallas kernels: 30.8 us -> 29.3 us
    pallas_call x1, Pallas kernels: 30.8 us -> 29.3 us  [on_device(): pl.pallas_call(functools.partial(layer_kernel, (peers, zs, rows, cols, ch...]
where the time goes in v6:
time: 30.9 us; the launch traced here: 30.3 us
  Pallas kernels  29.3 us (95%)
  local copies, waits for them, and re-layouts  0.97 us (3%)
    pallas_call x1, Pallas kernels, on_device(): pl.pallas_call(functools.partial(layer_kernel, (peers, zs, rows, cols, ch...  29.3 us
    unnamed x1, local copies, waits for them, and re-layouts  0.97 us

profile of v6, /device:TPU:32, one launch (start us, length us, event | category | flops | bytes accessed | tf_op | source)
XLA Modules:
  0.0 30.3 jit_solution(10494875273843843528)
XLA Ops:
  0.0 29.3 %layer.1 = bf16[2,32,16,512]{3,2,1,0:T(8,128)(2,1)S(1)} custom-call(bf16[2,32,16,512]{3,2,1,0:T(8,128)(2,1)} %frames_hbm.1, bf16[3,1536,512]{2,1,0:T(8,128)(2,1)} %bitcast.4, bf16[3,1536,512]{2,1,0:T(8,128)(2,1)} %bitcast.5, s32[1,512]{1,0:T(1,128)} %bitcast.6, f32[1,512]{1,0:T(1,128)} %bitcast.7, f32[32,16,512]{2,1,0:T(8,128)} %start_hbm.1), custom_call_target="tpu_custom_call" | custom-call | tf_op jit(solution)/shard_map/layer/pallas_call | solution.py:468
  29.3 1.0 %copy.8 = bf16[2,32,16,512]{3,2,1,0:T(8,128)(2,1)} copy(bf16[2,32,16,512]{3,2,1,0:T(8,128)(2,1)S(1)} %layer.1) | data formatting | bytes 2097152

commit v7 on v6

--- a/solution.py
+++ b/solution.py
@@ -391,24 +391,27 @@
                 beyond[d, f, 7:8, :] = jnp.where(sx == 1, row, 0.0)
                 beyond[d, f, 8 + rows : 9 + rows, :] = jnp.where(sx == 0, row, 0.0)
 
-    def finish():
+    def finish(at, count):
         for d, j, col in ((0, 0, 0), (1, 2, cols - 1)):
-            left_side = jnp.concatenate(
-                [
-                    jnp.concatenate([beyond[d, f, 7 + i : 7 + i + rows, :].astype(BF16) for i in range(3)], axis=-1)
-                    for f in range(2)
-                ],
-                axis=0,
-            )
+            parts = []
+            for f in range(2):
+                view = beyond.at[d, f, pl.ds(pl.multiple_of(at, 8), count + 16), :]
+                parts.append(
+                    jnp.concatenate([view[7 + i : 7 + i + count, :].astype(BF16) for i in range(3)], axis=-1)
+                )
+            left_side = jnp.concatenate(parts, axis=0)
             right_side = jnp.concatenate([w2[i, j * ch : (j + 1) * ch] for i in range(3)], axis=0)
-            acc[:, col, :] = acc[:, col, :] + jnp.dot(left_side, right_side, preferred_element_type=F32)
+            got = jnp.dot(left_side, right_side, preferred_element_type=F32)
+            for f in range(2):
+                spot = pl.ds(f * rows + at, count)
+                acc[spot, col, :] = acc[spot, col, :] + got[f * count : (f + 1) * count]
 
         def narrow(r, _):
             for f in range(2):
-                out[f, r] = acc[f * rows + r].astype(BF16)
+                out[f, at + r] = acc[f * rows + at + r].astype(BF16)
             return 0
 
-        lax.fori_loop(0, rows, narrow, 0, unroll=8)
+        lax.fori_loop(0, count, narrow, 0, unroll=8)
 
     drive_chunk(0)
     take(late)
@@ -448,10 +451,14 @@
     border_row()
     gather_chunk(3, every)
     flush()
-    for c in range(n):
+    beyond[:, :, 7:8, :] = jnp.zeros((2, 2, 1, ch), F32)
+    beyond[:, :, 8 + rows : 9 + rows, :] = jnp.zeros((2, 2, 1, ch), F32)
+    for c in range(n - 1):
         beyond_chunk(c)
+    finish(row_of(0, half), half)
+    beyond_chunk(n - 1)
     beyond_corners()
-    finish()
+    finish(row_of(half, rows), half)
     flush()
 
 

time: 30.9 us -> 31.3 us (1.013)
  the two profiles are of different devices: /device:TPU:32 before, /device:TPU:66 now
where the time goes in v7:
time: 31.3 us; the launch traced here: 31.2 us
  Pallas kernels  30.2 us (96%)
  local copies, waits for them, and re-layouts  0.97 us (3%)
    pallas_call x1, Pallas kernels, on_device(): pl.pallas_call(functools.partial(layer_kernel, (peers, zs, rows, cols, ch...  30.2 us
    unnamed x1, local copies, waits for them, and re-layouts  0.97 us

profile of v7, /device:TPU:66, one launch (start us, length us, event | category | flops | bytes accessed | tf_op | source)
XLA Modules:
  0.0 31.2 jit_solution(13093633645573571596)
XLA Ops:
  0.0 30.2 %layer.1 = bf16[2,32,16,512]{3,2,1,0:T(8,128)(2,1)S(1)} custom-call(bf16[2,32,16,512]{3,2,1,0:T(8,128)(2,1)} %frames_hbm.1, bf16[3,1536,512]{2,1,0:T(8,128)(2,1)} %bitcast.4, bf16[3,1536,512]{2,1,0:T(8,128)(2,1)} %bitcast.5, s32[1,512]{1,0:T(1,128)} %bitcast.6, f32[1,512]{1,0:T(1,128)} %bitcast.7, f32[32,16,512]{2,1,0:T(8,128)} %start_hbm.1), custom_call_target="tpu_custom_call" | custom-call | tf_op jit(solution)/shard_map/layer/pallas_call | solution.py:475
  30.2 1.0 %copy.8 = bf16[2,32,16,512]{3,2,1,0:T(8,128)(2,1)} copy(bf16[2,32,16,512]{3,2,1,0:T(8,128)(2,1)S(1)} %layer.1) | data formatting | bytes 2097152
